TPU v7x, 128 devices: a whole 4x4x4 slice. The times are simulated.
128 devices in a mesh: seq: 16 (over z, x_hi, core), exp: 8 (over y, x_lo).
Axes of the slice: x: 4 (x_hi: 2, x_lo: 2; x = x_hi * 2 + x_lo), y: 4, z: 4, core: 2. Of those that a mesh axis runs over, the one named last changes fastest.
Arguments:
- tokens: bfloat16 [524288, 1024], P(('seq', 'exp')), may hold values from -6 to 6
- norm_gain: float32 [1024], replicated, may hold values from 0.1 to 1.9
- slot_param: bfloat16 [1024, 256], replicated
- w_in: bfloat16 [64, 1024, 4096], P('exp', None, 'seq'), may hold values from -0.1875 to 0.1875
- w_out: bfloat16 [64, 4096, 1024], P('exp', 'seq'), may hold values from -0.09375 to 0.09375
Outputs:
- mixed: bfloat16 [524288, 1024], P(('seq', 'exp'))
All inputs are finite; a program needn't handle non-finite values.
Results may differ from a plain program's by a relative error of at most 0.02.
The roundings to bfloat16 on the way count: a program that leaves them out, or rounds other values in their place, can miss the bound.
Values may be sent and summed in bfloat16 or wider, within the bound.
A program may use at most 128 MiB of HBM per device.

v0:
```python
import jax
import jax.numpy as jnp
from jax import lax
from jax.sharding import PartitionSpec as P


def on_device(tokens, norm_gain, slot_param, w_in, w_out):
    n_exp = lax.axis_size("exp")
    slot_count = slot_param.shape[1]
    width = tokens.shape[1]
    group = slot_count // n_exp
    values = tokens.astype(jnp.float32)
    scale = lax.rsqrt(jnp.mean(values * values, axis=1, keepdims=True) + 1e-06)
    normed = (values * scale * norm_gain[None, :]).astype(jnp.bfloat16)
    logits = jnp.dot(normed, slot_param, preferred_element_type=jnp.float32)
    col_peak = lax.pmax(jnp.max(logits, axis=0), ("seq", "exp"))
    raw = jnp.exp(logits - col_peak[None, :])
    dispatch = raw.astype(jnp.bfloat16)
    weighted = lax.dot_general(
        dispatch, normed, (((0,), (0,)), ((), ())), preferred_element_type=jnp.float32
    )
    col_total = jnp.sum(raw, axis=0)
    group_sum, group_total = (
        lax.psum_scatter(weighted, "exp", scatter_dimension=0, tiled=True),
        lax.psum_scatter(col_total, "exp", scatter_dimension=0, tiled=True),
    )
    group_sum, group_total = lax.psum((group_sum, group_total), "seq")
    slot_in = (group_sum / group_total[:, None]).astype(jnp.bfloat16)
    local_experts = w_in.shape[0]
    grouped = slot_in.reshape(local_experts, group // local_experts, width)
    first = jnp.einsum("esd,edh->esh", grouped, w_in, preferred_element_type=jnp.float32)
    hidden_act = jax.nn.gelu(first, approximate=False).astype(jnp.bfloat16)
    partial_out = jnp.einsum(
        "esh,ehd->esd", hidden_act, w_out, preferred_element_type=jnp.float32
    ).reshape(group, width)
    group_out = lax.psum(partial_out.astype(jnp.bfloat16), "seq")
    slot_out = lax.all_gather(group_out, "exp", axis=0, tiled=True)
    row_peak = jnp.max(logits, axis=1, keepdims=True)
    expon = jnp.exp(logits - row_peak)
    combine = (expon / jnp.sum(expon, axis=1, keepdims=True)).astype(jnp.bfloat16)
    return jnp.dot(combine, slot_out, preferred_element_type=jnp.float32).astype(jnp.bfloat16)


def solution(mesh):
    in_specs = (P(("seq", "exp"), None), P(), P(), P("exp", None, "seq"), P("exp", "seq", None))
    out_specs = P(("seq", "exp"), None)
    return jax.shard_map(
        on_device, mesh=mesh, in_specs=in_specs, out_specs=out_specs, check_vma=False
    )
```

profile of v0, /device:TPU:1, one launch (start us, length us, event | category | flops | bytes accessed | tf_op | source)
XLA Modules:
  0.0 444.7 jit_solution(9162732727968139499)
XLA Ops:
  6.5 0.0 copy-start
  6.5 0.0 copy-start.3
  6.5 0.0 reduce-scatter.2.cloned.1.call-start
  6.5 0.0 copy-start.1
  6.5 5.2 %fusion = f32[4096]{0:T(1024)S(1)} fusion(bf16[4096,1024]{1,0:T(8,128)(2,1)} %param.5), kind=kLoop, calls=%fused_computation.2 | loop fusion | flops 12578816 | bytes 8404992 | tf_op jit(solution)/shard_map/reduce_sum | solution.py:13
  11.8 0.0 copy-done
  11.8 0.0 copy-done.3
  11.8 0.7 copy-done.1
  12.5 5.2 %fusion.89 = (f32[4096]{0:T(1024)S(1)}, f32[256]{0:T(256)S(1)}, f32[4096,256]{1,0:T(8,128)}) fusion(bf16[1024,256]{1,0:T(8,128)(2,1)S(1)} %copy-done, bf16[4096,1024]{1,0:T(8,128)(2,1)S(1)} %copy-done.1, f32[1024]{0:T(1024)S(1)} %copy-done.3, f32[4096]{0:T(1024)S(1)} %add_rsqrt_fusion), kind=kOutput, calls=%fused_computation.106 | convolution fusion | flops 2166353664 | bytes 13145088 | tf_op jit(solution)/shard_map/dot_general | solution.py:15
  17.7 68.6 %pmax.7 = f32[256]{0:T(256)S(1)} all-reduce(f32[256]{0:T(256)S(1)} %get-tuple-element.8), channel_id=1, replica_groups=mesh['seq'=16,'exp'=8] {'seq','exp'}, use_global_device_ids=true, to_apply=%region_4.0 | all-reduce | flops 256 | bytes 2048 | tf_op jit(solution)/shard_map/pmax | solution.py:16
  86.3 8.9 %fusion.6 = f32[256,1024]{1,0:T(8,128)} fusion(bf16[4096,1024]{1,0:T(8,128)(2,1)} %param.5, f32[1024]{0:T(1024)S(1)} %copy-done.3, f32[4096]{0:T(1024)S(1)} %add_rsqrt_fusion, f32[4096,256]{1,0:T(8,128)} %get-tuple-element.11, f32[256]{0:T(256)S(1)} %pmax.7), kind=kOutput, calls=%fused_computation.12 | convolution fusion | flops 2166358016 | bytes 13652992 | tf_op jit(solution)/shard_map/dot_general | solution.py:19
  95.2 0.0 copy-start.4
  95.2 0.0 reduce-scatter.2.cloned.1.call-update
  95.3 0.0 all-reduce.4.cloned.1.call-start
  95.3 33.1 %reduce-scatter.2.cloned.1.call-done = f32[32,1024]{1,0:T(8,128)} async-done(((f32[256,1024]{1,0:T(8,128)}), f32[32,1024]{1,0:T(8,128)}) %reduce-scatter.2.cloned.1.call-update) | async-done | bytes 131088 | tf_op jit(solution)/shard_map/reduce_scatter | solution.py:24
  128.4 0.0 all-reduce.4.cloned.1.call-update
  128.5 0.0 all-reduce.6.cloned.1.call-start
  128.5 3.4 fusion.3
  131.9 0.0 copy-done.4
  131.9 0.6 dynamic-slice
  133.1 14.9 %all-reduce = f32[256]{0:T(256)S(1)} all-reduce(f32[256]{0:T(256)S(1)} %get-tuple-element.6), channel_id=3, replica_groups=mesh['seq'=16,'exp'=8] {'exp'}, use_global_device_ids=true, to_apply=%region_8.0.clone | all-reduce | flops 256 | bytes 2048
  148.0 0.1 dynamic-slice.1
  148.1 40.3 %psum.22 = f32[32]{0:T(128)S(1)} all-reduce(f32[32]{0:T(128)S(1)} %dynamic-slice.1), channel_id=1, replica_groups=mesh['seq'=16,'exp'=8] {'seq'}, use_global_device_ids=true, to_apply=%region_9.0 | all-reduce | flops 32 | bytes 256 | tf_op jit(solution)/shard_map/psum | solution.py:27
  188.3 85.0 %all-reduce.4.cloned.1.call-done = f32[32,1024]{1,0:T(8,128)} async-done(((f32[32,1024]{1,0:T(8,128)}), f32[32,1024]{1,0:T(8,128)}) %all-reduce.4.cloned.1.call-update) | async-done | bytes 131088 | tf_op jit(solution)/shard_map/psum | solution.py:27
  273.4 1.0 divide_convert_fusion.2
  274.4 0.0 copy-start.2
  274.4 3.0 fusion.55
  277.4 0.4 copy-done.2
  277.8 0.7 convolution_convert_fusion.1
  278.5 0.7 convert_element_type.34
  279.2 0.0 all-reduce.6.cloned.1.call-update
  279.2 128.7 %all-reduce.6.cloned.1.call-done = bf16[32,1024]{1,0:T(8,128)(2,1)} async-done(((bf16[32,1024]{1,0:T(8,128)(2,1)}), bf16[32,1024]{1,0:T(8,128)(2,1)}) %all-reduce.6.cloned.1.call-update) | async-done | bytes 65552 | tf_op jit(solution)/shard_map/psum | solution.py:36
  407.9 23.9 %all_gather.3 = bf16[256,1024]{1,0:T(8,128)(2,1)S(1)} all-gather(bf16[32,1024]{1,0:T(8,128)(2,1)} %all-reduce.6.cloned.1.call-done), channel_id=1, replica_groups=mesh['seq'=16,'exp'=8] {'exp'}, dimensions={0}, use_global_device_ids=true | all-gather | bytes 589824 | tf_op jit(solution)/shard_map/all_gather | solution.py:37
  431.8 6.4 %convolution_convert_fusion = bf16[4096,1024]{1,0:T(8,128)(2,1)} fusion(bf16[256,1024]{1,0:T(8,128)(2,1)S(1)} %all_gather.3, f32[4096,256]{1,0:T(8,128)} %get-tuple-element.11, f32[4096]{0:T(1024)S(1)} %get-tuple-element.5, f32[4096]{0:T(1024)S(1)} %get-tuple-element.7), kind=kOutput, calls=%fused_computation.5 | convolution fusion | flops 2154823680 | bytes 13139968 | tf_op jit(solution)/shard_map/dot_general | solution.py:41
  (2 shorter events, 0.0 us)
Async XLA Ops:
  6.5 5.3 %copy-start = (bf16[1024,256]{1,0:T(8,128)(2,1)S(1)}, bf16[1024,256]{1,0:T(8,128)(2,1)}, u32[]{:S(2)}) copy-start(bf16[1024,256]{1,0:T(8,128)(2,1)} %param.7) | copy-start | bytes 1572868
  6.5 5.3 %copy-start.3 = (f32[1024]{0:T(1024)S(1)}, f32[1024]{0:T(1024)}, u32[]{:S(2)}) copy-start(f32[1024]{0:T(1024)} %param.6) | copy-start | bytes 12292
  6.5 121.9 %reduce-scatter.2.cloned.1.call-start = ((), (), s32[]{:S(2)}) async-start(), calls=%async_computation.1 | async-start | bytes 1179648 | tf_op jit(solution)/shard_map/reduce_scatter | solution.py:24
  6.5 6.0 %copy-start.1 = (bf16[4096,1024]{1,0:T(8,128)(2,1)S(1)}, bf16[4096,1024]{1,0:T(8,128)(2,1)}, u32[]{:S(2)}) copy-start(bf16[4096,1024]{1,0:T(8,128)(2,1)} %param.5) | copy-start | bytes 25165828
  95.2 36.6 %copy-start.4 = (u32[128]{0:T(128)S(1)}, u32[128]{0:T(128)}, u32[]{:S(2)}) copy-start(u32[128]{0:T(128)} %constant.70) | copy-start | bytes 1540
  95.3 178.1 %all-reduce.4.cloned.1.call-start = ((), (), s32[]{:S(2)}) async-start(), calls=%async_computation.2 | async-start | bytes 262144 | tf_op jit(solution)/shard_map/psum | solution.py:27
  128.5 279.4 %all-reduce.6.cloned.1.call-start = ((), (), s32[]{:S(2)}) async-start(), calls=%async_computation.3 | async-start | bytes 131072 | tf_op jit(solution)/shard_map/psum | solution.py:36
  274.4 3.5 copy-start.2
Sparse Core Ops, SparseCore 0:
  95.4 33.0 reduce-scatter.1
  130.9 142.4 all-reduce.3
  279.3 128.5 all-reduce.5
where the time goes:
time: 452 us; the launch traced here: 445 us
  waiting for transfers between devices  247 us (55%)
  blocking collectives  148 us (33%)
  matrix products  24.2 us (5%)
  between operations  13.8 us (3%)
  other arithmetic  9.59 us (2%)
    psum x1, waiting for transfers between devices, on_device(): group_out = lax.psum(partial_out.astype(jnp.bfloat16), 'seq')  129 us
    psum x1, waiting for transfers between devices, on_device(): group_sum, group_total = lax.psum((group_sum, group_total), 'seq')  85 us
    pmax x1, blocking collectives, on_device(): col_peak = lax.pmax(jnp.max(logits, axis=0), ('seq', 'exp'))  68.6 us
    psum x1, blocking collectives, on_device(): group_sum, group_total = lax.psum((group_sum, group_total), 'seq')  40.3 us
    reduce_scatter x1, waiting for transfers between devices, on_device(): lax.psum_scatter(weighted, 'exp', scatter_dimension=0, tiled=True)  33.1 us
    all_gather x1, blocking collectives, on_device(): slot_out = lax.all_gather(group_out, 'exp', axis=0, tiled=True)  23.9 us
    unnamed x1, blocking collectives  14.9 us
  transfers between devices with their start and end apart: 3, of which 3 were waited for; matrix products, arithmetic and copies ran while one was open for 1% of the time, Pallas kernels for 0%

commit v1 on v0

v1 whole, which is shorter than its diff:
```python
import functools

import jax
import jax.numpy as jnp
from jax import lax
from jax.experimental import pallas as pl
from jax.experimental.pallas import tpu as pltpu
from jax.sharding import PartitionSpec as P

MESH = pl.DeviceIdType.MESH
F32 = jnp.float32
BF16 = jnp.bfloat16
PLANE = 16
COLUMN = 8
META = 128


def split3(v):
    hi = v.astype(BF16).astype(F32)
    rest = v - hi
    mid = rest.astype(BF16).astype(F32)
    return hi, mid, rest - mid


def meta_block(peak, total):
    rows = peak.shape[0]
    lane = lax.broadcasted_iota(jnp.int32, (rows, META), 1)
    out = jnp.zeros((rows, META), F32)
    for i, part in enumerate(split3(peak) + split3(total)):
        out = jnp.where(lane == i, part, out)
    return out.astype(BF16)


def read_meta(block):
    v = block.astype(F32)
    peak = v[:, 0:1] + v[:, 1:2] + v[:, 2:3]
    total = v[:, 3:4] + v[:, 4:5] + v[:, 5:6]
    return peak, total


def moe_kernel(
    tok, gain_ref, slot_ref, win_hbm, wout_hbm,
    comb_hbm, g_ref,
    xbuf, lbuf, dbuf, cbuf, win, wout, mx, acc, colbuf,
    s0, r0, s1, r1, s2, r2, sl, hbuf, xs, xr, s4, r4,
    tsem, wsem, csem,
    core_send, core_recv, plane_send, plane_recv, column_send, column_recv,
    back_send, back_recv, gather_send, gather_recv, fwd_send, fwd_recv,
):
    tokens, width = xbuf.shape
    slots = slot_ref.shape[1]
    half = width // 2
    group = sl.shape[1]
    piece = group // 2
    local_experts = win.shape[0]
    per = group // local_experts
    hidden = win.shape[2]
    chunks = tsem.shape[0]
    rows = tokens // chunks

    s = lax.axis_index("seq")
    e = lax.axis_index("exp")
    c = lax.rem(s, 2)
    xh = lax.rem(s // 2, 2)
    z0 = lax.rem(s // 4, 2)
    z1 = s // 8
    xl = lax.rem(e, 2)
    y0 = lax.rem(e // 2, 2)
    y1 = e // 4

    def bit(b, k, i):
        return 1 - b if (k >> i) & 1 else b

    def plane_peer(k):
        pe = (bit(y1, k, 2) * 2 + bit(y0, k, 1)) * 2 + bit(xl, k, 0)
        ph = bit(xh, k, 3)
        ps = ((z1 * 2 + z0) * 2 + ph) * 2 + c
        row = pl.multiple_of(pe * group + ph * piece, piece)
        return (ps, pe), row

    def column_peer(k):
        ps = ((bit(z1, k, 2) * 2 + bit(z0, k, 1)) * 2 + bit(xh, k, 0)) * 2 + c
        return (ps, e)

    partner = (s + 1 - 2 * c, e)

    def remote(src, dst, send, recv, device):
        return pltpu.make_async_remote_copy(
            src_ref=src, dst_ref=dst, send_sem=send, recv_sem=recv,
            device_id=device, device_id_type=MESH,
        )

    def token_copy(i):
        at = pl.ds(pl.multiple_of(i * rows, rows), rows)
        return pltpu.make_async_copy(tok.at[at], xbuf.at[at], tsem.at[i])

    for i in range(chunks):
        token_copy(i).start()
    barrier = pltpu.get_barrier_semaphore()
    greeted = [partner]
    greeted += [plane_peer(k)[0] for k in range(1, PLANE)]
    greeted += [column_peer(k) for k in range(2, COLUMN)]
    for device in greeted:
        pl.semaphore_signal(barrier, inc=1, device_id=device, device_id_type=MESH)
    win_copy = pltpu.make_async_copy(win_hbm, win, wsem.at[0])
    wout_copy = pltpu.make_async_copy(wout_hbm, wout, wsem.at[1])

    gain = gain_ref[...]
    mx[...] = jnp.full(mx.shape, -jnp.inf, F32)

    @pl.loop(0, chunks)
    def _(i):
        token_copy(i).wait()
        base = i * rows

        @pl.loop(0, rows // 32, unroll=4)
        def _(j):
            at = pl.ds(pl.multiple_of(base + j * 32, 32), 32)
            v = xbuf[at, :].astype(F32)
            scale = lax.rsqrt(jnp.mean(v * v, axis=1, keepdims=True) + 1e-06)
            xbuf[at, :] = (v * scale * gain).astype(BF16)

        at = pl.ds(pl.multiple_of(base, rows), rows)
        logits = jnp.dot(xbuf[at, :], slot_ref[...], preferred_element_type=F32)
        lbuf[at, :] = logits
        mx[...] = jnp.maximum(mx[...], jnp.max(logits.reshape(rows // 8, 8, slots), axis=0))

    win_copy.start()
    wout_copy.start()
    peak = jnp.max(mx[...], axis=0, keepdims=True)

    def dispatch(i, total):
        at = pl.ds(pl.multiple_of(i * 64, 64), 64)
        raw = jnp.exp(lbuf[at, :] - peak)
        dbuf[at, :] = raw.astype(BF16)
        return total + jnp.sum(raw.reshape(8, 8, slots), axis=0)

    total = lax.fori_loop(0, tokens // 64, dispatch, jnp.zeros((8, slots), F32), unroll=4)
    total = jnp.sum(total, axis=0, keepdims=True)
    line = lax.broadcasted_iota(jnp.int32, (META, slots), 0)
    both = jnp.where(line == 0, peak, jnp.where(line == 1, total, 0.0))
    colbuf[...] = jnp.transpose(both)
    my_meta = meta_block(colbuf[:, 0:1], colbuf[:, 1:2])

    depth = 1024 if tokens % 1024 == 0 else tokens

    def weigh(h):
        acc[...] = jnp.zeros(acc.shape, F32)
        cols = pl.ds(pl.multiple_of(h * half, half), half)

        @pl.loop(0, tokens // depth)
        def _(i):
            at = pl.ds(pl.multiple_of(i * depth, depth), depth)
            acc[...] += lax.dot_general(
                dbuf[at, :], xbuf[at, cols], (((0,), (0,)), ((), ())),
                preferred_element_type=F32,
            )

    pl.semaphore_wait(barrier, len(greeted))
    weigh(1 - c)
    s0[:, :half] = acc[...].astype(BF16)
    s0[:, half:] = my_meta
    first_copy = remote(s0, r0, core_send.at[0], core_recv.at[0], partner)
    first_copy.start()
    weigh(c)
    first_copy.wait()

    def chip_piece(row):
        at = pl.ds(row, piece)
        mine, my_total = colbuf[at, 0:1], colbuf[at, 1:2]
        other, other_total = read_meta(r0[at, half:])
        joint = jnp.maximum(mine, other)
        wa, wb = jnp.exp(mine - joint), jnp.exp(other - joint)
        s1[at, :half] = (acc[at, :] * wa + r0[at, :half].astype(F32) * wb).astype(BF16)
        s1[at, half:] = meta_block(joint, my_total * wa + other_total * wb)

    order = sorted(range(1, PLANE), key=lambda k: -bin(k).count("1"))
    plane_copies = {}
    for k in order:
        device, row = plane_peer(k)
        chip_piece(row)
        at = pl.ds(row, piece)
        plane_copies[k] = remote(s1.at[at], r1.at[k], plane_send.at[k], plane_recv.at[k], device)
        plane_copies[k].start()
    my_row = plane_peer(0)[1]
    chip_piece(my_row)

    @pl.loop(0, tokens // 32, unroll=4)
    def _(i):
        at = pl.ds(pl.multiple_of(i * 32, 32), 32)
        v = lbuf[at, :]
        ex = jnp.exp(v - jnp.max(v, axis=1, keepdims=True))
        cbuf[at, :] = (ex / jnp.sum(ex, axis=1, keepdims=True)).astype(BF16)

    comb_copy = pltpu.make_async_copy(cbuf, comb_hbm, csem.at[0])
    comb_copy.start()

    def merge(blocks):
        metas = [read_meta(b[:, half:]) for b in blocks]
        joint = functools.reduce(jnp.maximum, [m for m, _ in metas])
        scales = [jnp.exp(m - joint) for m, _ in metas]
        out = sum(b[:, :half].astype(F32) * w for b, w in zip(blocks, scales))
        return out, joint, sum(t * w for (_, t), w in zip(metas, scales))

    for k in order:
        plane_copies[k].wait_recv()
    summed, joint, total_k = merge([s1[pl.ds(my_row, piece), :]] + [r1[k] for k in range(1, PLANE)])
    s2[:, :half] = summed.astype(BF16)
    s2[:, half:] = meta_block(joint, total_k)

    column_copies = {}
    for k in sorted(range(1, COLUMN), key=lambda k: -bin(k).count("1")):
        column_copies[k] = remote(s2, r2.at[k], column_send.at[k], column_recv.at[k], column_peer(k))
        column_copies[k].start()
    for k in range(1, COLUMN):
        column_copies[k].wait_recv()
    for odd in range(2):
        blocks = [s2[...] if k == 0 else r2[k] for k in range(odd, COLUMN, 2)]
        out, _, tot = merge(blocks)
        at = pl.multiple_of((1 - xh if odd else xh) * piece, piece)
        sl[c, pl.ds(at, piece), :] = (out / tot).astype(BF16)
    in_copy = remote(sl.at[c], sl.at[c], core_send.at[1], core_recv.at[1], partner)
    in_copy.start()
    win_copy.wait()
    wout_copy.wait()
    in_copy.wait()

    owner = lax.broadcasted_iota(jnp.int32, (group, hidden), 0) // per
    first = jnp.zeros((group, hidden), F32)
    for x in range(local_experts):
        y = jnp.dot(sl[0], win[x, :half, :], preferred_element_type=F32)
        y += jnp.dot(sl[1], win[x, half:, :], preferred_element_type=F32)
        first = jnp.where(owner == x, y, first)
    act = 0.5 * first * (1.0 + lax.erf(first * 0.7071067811865476))
    for x in range(local_experts):
        hbuf[:, x * hidden:(x + 1) * hidden] = jnp.where(owner == x, act, 0.0).astype(BF16)

    def project(h):
        cols = pl.ds(pl.multiple_of(h * half, half), half)
        return sum(
            jnp.dot(hbuf[:, x * hidden:(x + 1) * hidden], wout[x, :, cols], preferred_element_type=F32)
            for x in range(local_experts)
        )

    xs[...] = project(1 - c).astype(BF16)
    out_copy = remote(xs, xr, core_send.at[2], core_recv.at[2], partner)
    out_copy.start()
    own = project(c)
    out_copy.wait()
    s4[...] = (own + xr[...].astype(F32)).astype(BF16)

    back_copies = {}
    for k in sorted(range(1, COLUMN), key=lambda k: -bin(k).count("1")):
        at = pl.ds(pl.multiple_of(bit(xh, k, 0) * piece, piece), piece)
        back_copies[k] = remote(s4.at[at], r4.at[k], back_send.at[k], back_recv.at[k], column_peer(k))
        back_copies[k].start()
    mine = s4[pl.ds(pl.multiple_of(xh * piece, piece), piece), :].astype(F32)
    for k in range(1, COLUMN):
        back_copies[k].wait_recv()
        mine += r4[k].astype(F32)
    at = pl.ds(my_row, piece)
    g_ref[c, at, :] = mine.astype(BF16)

    gathers = {}
    for k in order:
        gathers[k] = remote(
            g_ref.at[c, at], g_ref.at[c, at], gather_send.at[k], gather_recv.at[k], plane_peer(k)[0]
        )
        gathers[k].start()
    forwards = []
    for k in [0] + order[::-1]:
        if k:
            gathers[k].wait_recv()
        there = pl.ds(plane_peer(k)[1], piece)
        forwards.append(
            remote(g_ref.at[c, there], g_ref.at[c, there], fwd_send.at[k], fwd_recv.at[k], partner)
        )
        forwards[-1].start()
    for copy in forwards:
        copy.wait()
    for copies in (plane_copies, column_copies, back_copies, gathers):
        for copy in copies.values():
            copy.wait_send()
    comb_copy.wait()


def mix_kernel(c_ref, g_ref, o_ref):
    half = g_ref.shape[2]
    for h in range(2):
        o_ref[:, h * half:(h + 1) * half] = jnp.dot(
            c_ref[...], g_ref[h], preferred_element_type=F32
        ).astype(BF16)


def on_device(tokens, norm_gain, slot_param, w_in, w_out):
    n, width = tokens.shape
    slots = slot_param.shape[1]
    half = width // 2
    group = slots // lax.axis_size("exp")
    piece = group // 2
    hidden = w_in.shape[2]
    chunks = 8
    wide = half + META
    dma = pltpu.SemaphoreType.DMA
    anywhere = pl.BlockSpec(memory_space=pl.ANY)
    vmem = pl.BlockSpec(memory_space=pltpu.VMEM)
    combine, gathered = pl.pallas_call(
        moe_kernel,
        out_shape=(
            jax.ShapeDtypeStruct((n, slots), BF16),
            jax.ShapeDtypeStruct((2, slots, half), BF16),
        ),
        in_specs=[anywhere, vmem, vmem, anywhere, anywhere],
        out_specs=(anywhere, vmem),
        scratch_shapes=[
            pltpu.VMEM((n, width), BF16),
            pltpu.VMEM((n, slots), F32),
            pltpu.VMEM((n, slots), BF16),
            pltpu.VMEM((n, slots), BF16),
            pltpu.VMEM(w_in.shape, BF16),
            pltpu.VMEM(w_out.shape, BF16),
            pltpu.VMEM((8, slots), F32),
            pltpu.VMEM((slots, half), F32),
            pltpu.VMEM((slots, META), F32),
            pltpu.VMEM((slots, wide), BF16),
            pltpu.VMEM((slots, wide), BF16),
            pltpu.VMEM((slots, wide), BF16),
            pltpu.VMEM((PLANE, piece, wide), BF16),
            pltpu.VMEM((piece, wide), BF16),
            pltpu.VMEM((COLUMN, piece, wide), BF16),
            pltpu.VMEM((2, group, half), BF16),
            pltpu.VMEM((group, w_in.shape[0] * hidden), BF16),
            pltpu.VMEM((group, half), BF16),
            pltpu.VMEM((group, half), BF16),
            pltpu.VMEM((group, half), BF16),
            pltpu.VMEM((COLUMN, piece, half), BF16),
            dma((chunks,)),
            dma((2,)),
            dma((1,)),
            dma((3,)), dma((3,)),
            dma((PLANE,)), dma((PLANE,)),
            dma((COLUMN,)), dma((COLUMN,)),
            dma((COLUMN,)), dma((COLUMN,)),
            dma((PLANE,)), dma((PLANE,)),
            dma((PLANE,)), dma((PLANE,)),
        ],
        compiler_params=pltpu.CompilerParams(
            collective_id=0, has_side_effects=True, vmem_limit_bytes=48 * 2**20
        ),
        name="moe",
    )(tokens, norm_gain.reshape(1, width), slot_param, w_in, w_out)
    block = n // 8
    return pl.pallas_call(
        mix_kernel,
        grid=(8,),
        out_shape=jax.ShapeDtypeStruct((n, width), BF16),
        in_specs=[
            pl.BlockSpec((block, slots), lambda i: (i, 0)),
            pl.BlockSpec((2, slots, half), lambda i: (0, 0, 0)),
        ],
        out_specs=pl.BlockSpec((block, width), lambda i: (i, 0)),
        name="mix",
    )(combine, gathered)


def solution(mesh):
    in_specs = (P(("seq", "exp"), None), P(), P(), P("exp", None, "seq"), P("exp", "seq", None))
    out_specs = P(("seq", "exp"), None)
    return jax.shard_map(
        on_device, mesh=mesh, in_specs=in_specs, out_specs=out_specs, check_vma=False
    )
```

time: 452 us -> 75.2 us (0.17); the launches traced: 445 us -> 74.9 us
  waiting for transfers between devices: 247 us -> 0 us
  blocking collectives: 148 us -> 0 us
  Pallas kernels: 0 us -> 71 us
  matrix products: 24.2 us -> 0 us
  between operations: 13.8 us -> 0.02 us
  other arithmetic: 9.59 us -> 0 us
    psum x2 -> x0, waiting for transfers between devices: 214 us -> none  [the longest x1 129 us: on_device(): group_out = lax.psum(partial_out.astype(jnp.bfloat16), 'seq')]
    pallas_call x0 -> x2, Pallas kernels: none -> 71 us  [the longest x1 62.7 us: on_device(): pl.pallas_call(moe_kernel, out_shape=(jax.ShapeDtypeStruct((n, slots), BF...]
    pmax x1 -> x0, blocking collectives: 68.6 us -> none  [on_device(): col_peak = lax.pmax(jnp.max(logits, axis=0), ('seq', 'exp'))]
    psum x1 -> x0, blocking collectives: 40.3 us -> none  [on_device(): group_sum, group_total = lax.psum((group_sum, group_total), 'seq')]
    reduce_scatter x1 -> x0, waiting for transfers between devices: 33.1 us -> none  [on_device(): lax.psum_scatter(weighted, 'exp', scatter_dimension=0, tiled=True)]
    dot_general x5 -> x0, matrix products: 24.2 us -> none  [the longest x1 8.91 us: on_device(): lax.dot_general(dispatch, normed, (((0,), (0,)), ((), ())), preferred_ele...]
    all_gather x1 -> x0, blocking collectives: 23.9 us -> none  [on_device(): slot_out = lax.all_gather(group_out, 'exp', axis=0, tiled=True)]
    unnamed x1 -> x0, blocking collectives: 14.9 us -> none
  transfers between devices with their start and end apart: 3 -> 0, of which waited for: 3 -> 0; matrix products, arithmetic and copies ran while one was open for 1% -> 0% of each run, Pallas kernels for 0% -> 0%
where the time goes in v1:
time: 75.2 us; the launch traced here: 74.9 us
  Pallas kernels  71 us (94%)
  local copies, waits for them, and re-layouts  3.84 us (5%)
    pallas_call x1, Pallas kernels, on_device(): pl.pallas_call(moe_kernel, out_shape=(jax.ShapeDtypeStruct((n, slots), BF...  62.7 us
    pallas_call x1, Pallas kernels, on_device(): pl.pallas_call(mix_kernel, grid=(8,), out_shape=jax.ShapeDtypeStruct((n,...  8.3 us
    unnamed x8, local copies, waits for them, and re-layouts  3.84 us

profile of v1, /device:TPU:1, one launch (start us, length us, event | category | flops | bytes accessed | tf_op | source)
XLA Modules:
  0.0 74.9 jit_solution(11715580909356547638)
XLA Ops:
  0.0 0.0 copy-start.1
  0.0 1.0 %copy-done.1 = bf16[1024,256]{1,0:T(8,128)(2,1)S(1)} copy-done((bf16[1024,256]{1,0:T(8,128)(2,1)S(1)}, bf16[1024,256]{1,0:T(8,128)(2,1)}, u32[]{:S(2)}) %copy-start.1) | copy-done | bytes 524312
  1.0 0.0 copy-start.3
  1.0 0.7 copy-done.3
  1.7 62.7 %moe.1 = (bf16[4096,256]{1,0:T(8,128)(2,1)S(1)}, bf16[2,256,512]{2,1,0:T(8,128)(2,1)S(1)}) custom-call(bf16[4096,1024]{1,0:T(8,128)(2,1)} %tok.1, f32[1,1024]{1,0:T(1,128)S(1)} %bitcast.1, bf16[1024,256]{1,0:T(8,128)(2,1)S(1)} %copy-done.1, bf16[8,1024,256]{2,1,0:T(8,128)(2,1)} %win_hbm.1, bf16[8,256,1024]{2,1,0:T(8,128)(2,1)} %wout_hbm.1), custom_call_target="tpu_custom_call" | custom-call | tf_op jit(solution)/shard_map/moe/pallas_call | solution.py:307
  64.4 0.0 copy-start
  64.4 1.3 %copy-done = bf16[4096,256]{1,0:T(8,128)(2,1)} copy-done((bf16[4096,256]{1,0:T(8,128)(2,1)}, bf16[4096,256]{1,0:T(8,128)(2,1)S(1)}, u32[]{:S(2)}) %copy-start) | copy-done | bytes 2097176
  65.8 0.0 copy-start.2
  65.8 0.8 %copy-done.2 = bf16[2,256,512]{2,1,0:T(8,128)(2,1)} copy-done((bf16[2,256,512]{2,1,0:T(8,128)(2,1)}, bf16[2,256,512]{2,1,0:T(8,128)(2,1)S(1)}, u32[]{:S(2)}) %copy-start.2) | copy-done | bytes 524312
  66.6 8.3 %mix.1 = bf16[4096,1024]{1,0:T(8,128)(2,1)} custom-call(bf16[4096,256]{1,0:T(8,128)(2,1)} %copy-done, bf16[2,256,512]{2,1,0:T(8,128)(2,1)} %copy-done.2), custom_call_target="tpu_custom_call" | custom-call | tf_op jit(solution)/shard_map/mix/pallas_call | solution.py:353
Async XLA Ops:
  0.0 1.0 %copy-start.1 = (bf16[1024,256]{1,0:T(8,128)(2,1)S(1)}, bf16[1024,256]{1,0:T(8,128)(2,1)}, u32[]{:S(2)}) copy-start(bf16[1024,256]{1,0:T(8,128)(2,1)} %slot_ref.1) | copy-start | bytes 1572868
  1.0 0.7 copy-start.3
  64.4 1.3 %copy-start = (bf16[4096,256]{1,0:T(8,128)(2,1)}, bf16[4096,256]{1,0:T(8,128)(2,1)S(1)}, u32[]{:S(2)}) copy-start(bf16[4096,256]{1,0:T(8,128)(2,1)S(1)} %get-tuple-element.7.c_ref) | copy-start | bytes 6291460
  65.8 0.8 %copy-start.2 = (bf16[2,256,512]{2,1,0:T(8,128)(2,1)}, bf16[2,256,512]{2,1,0:T(8,128)(2,1)S(1)}, u32[]{:S(2)}) copy-start(bf16[2,256,512]{2,1,0:T(8,128)(2,1)S(1)} %get-tuple-element.8.g_ref) | copy-start | bytes 1572868

commit v2 on v1

--- a/solution.py
+++ b/solution.py
@@ -39,11 +39,11 @@
 
 
 def moe_kernel(
-    tok, gain_ref, slot_ref, win_hbm, wout_hbm,
-    comb_hbm, g_ref,
-    xbuf, lbuf, dbuf, cbuf, win, wout, mx, acc, colbuf,
+    tok, gain_hbm, slot_hbm, win_hbm, wout_hbm,
+    cbuf, g_ref,
+    raw, xbuf, pair, lbuf, dbuf, win, wout, gain_ref, slot_ref, mx, acc, colbuf,
     s0, r0, s1, r1, s2, r2, sl, hbuf, xs, xr, s4, r4,
-    tsem, wsem, csem,
+    tsem, wsem,
     core_send, core_recv, plane_send, plane_recv, column_send, column_recv,
     back_send, back_recv, gather_send, gather_recv, fwd_send, fwd_recv,
 ):
@@ -92,9 +92,14 @@
 
     def token_copy(i):
         at = pl.ds(pl.multiple_of(i * rows, rows), rows)
-        return pltpu.make_async_copy(tok.at[at], xbuf.at[at], tsem.at[i])
-
-    for i in range(chunks):
+        return pltpu.make_async_copy(tok.at[at], raw.at[at], tsem.at[i])
+
+    token_copy(0).start()
+    gain_copy = pltpu.make_async_copy(gain_hbm, gain_ref, wsem.at[2])
+    slot_copy = pltpu.make_async_copy(slot_hbm, slot_ref, wsem.at[3])
+    gain_copy.start()
+    slot_copy.start()
+    for i in range(1, chunks):
         token_copy(i).start()
     barrier = pltpu.get_barrier_semaphore()
     greeted = [partner]
@@ -105,64 +110,72 @@
     win_copy = pltpu.make_async_copy(win_hbm, win, wsem.at[0])
     wout_copy = pltpu.make_async_copy(wout_hbm, wout, wsem.at[1])
 
+    gain_copy.wait()
+    slot_copy.wait()
     gain = gain_ref[...]
     mx[...] = jnp.full(mx.shape, -jnp.inf, F32)
 
-    @pl.loop(0, chunks)
-    def _(i):
-        token_copy(i).wait()
-        base = i * rows
-
-        @pl.loop(0, rows // 32, unroll=4)
-        def _(j):
-            at = pl.ds(pl.multiple_of(base + j * 32, 32), 32)
-            v = xbuf[at, :].astype(F32)
+    def norm(i, slot):
+        for q in range(rows // 32):
+            at = pl.ds(pl.multiple_of(i * rows + q * 32, 32), 32)
+            v = raw[at, :].astype(F32)
             scale = lax.rsqrt(jnp.mean(v * v, axis=1, keepdims=True) + 1e-06)
-            xbuf[at, :] = (v * scale * gain).astype(BF16)
-
-        at = pl.ds(pl.multiple_of(base, rows), rows)
-        logits = jnp.dot(xbuf[at, :], slot_ref[...], preferred_element_type=F32)
+            normed = (v * scale * gain).astype(BF16)
+            xbuf[at, :] = normed
+            pair[slot][q * 32:(q + 1) * 32, :] = normed
+
+    def project_slots(i, slot):
+        at = pl.ds(pl.multiple_of(i * rows, rows), rows)
+        logits = jnp.dot(pair[slot][...], slot_ref[...], preferred_element_type=F32)
         lbuf[at, :] = logits
         mx[...] = jnp.maximum(mx[...], jnp.max(logits.reshape(rows // 8, 8, slots), axis=0))
+
+    token_copy(0).wait()
+    norm(0, 0)
+
+    @pl.loop(0, chunks // 2 - 1)
+    def _(i):
+        for slot in range(2):
+            token_copy(2 * i + slot + 1).wait()
+            norm(2 * i + slot + 1, 1 - slot)
+            project_slots(2 * i + slot, slot)
+
+    token_copy(chunks - 1).wait()
+    norm(chunks - 1, 1)
+    project_slots(chunks - 2, 0)
+    project_slots(chunks - 1, 1)
 
     win_copy.start()
     wout_copy.start()
     peak = jnp.max(mx[...], axis=0, keepdims=True)
 
+    step = min(256, tokens)
+
     def dispatch(i, total):
-        at = pl.ds(pl.multiple_of(i * 64, 64), 64)
-        raw = jnp.exp(lbuf[at, :] - peak)
-        dbuf[at, :] = raw.astype(BF16)
-        return total + jnp.sum(raw.reshape(8, 8, slots), axis=0)
-
-    total = lax.fori_loop(0, tokens // 64, dispatch, jnp.zeros((8, slots), F32), unroll=4)
+        at = pl.ds(pl.multiple_of(i * step, step), step)
+        ex = jnp.exp(lbuf[at, :] - peak)
+        dbuf[at, :] = ex.astype(BF16)
+        return total + jnp.sum(ex.reshape(step // 8, 8, slots), axis=0)
+
+    total = lax.fori_loop(0, tokens // step, dispatch, jnp.zeros((8, slots), F32))
     total = jnp.sum(total, axis=0, keepdims=True)
     line = lax.broadcasted_iota(jnp.int32, (META, slots), 0)
     both = jnp.where(line == 0, peak, jnp.where(line == 1, total, 0.0))
     colbuf[...] = jnp.transpose(both)
     my_meta = meta_block(colbuf[:, 0:1], colbuf[:, 1:2])
 
-    depth = 1024 if tokens % 1024 == 0 else tokens
-
     def weigh(h):
-        acc[...] = jnp.zeros(acc.shape, F32)
         cols = pl.ds(pl.multiple_of(h * half, half), half)
-
-        @pl.loop(0, tokens // depth)
-        def _(i):
-            at = pl.ds(pl.multiple_of(i * depth, depth), depth)
-            acc[...] += lax.dot_general(
-                dbuf[at, :], xbuf[at, cols], (((0,), (0,)), ((), ())),
-                preferred_element_type=F32,
-            )
-
+        return lax.dot_general(
+            dbuf[...], xbuf[:, cols], (((0,), (0,)), ((), ())), preferred_element_type=F32
+        )
+
+    s0[:, :half] = weigh(1 - c).astype(BF16)
+    s0[:, half:] = my_meta
     pl.semaphore_wait(barrier, len(greeted))
-    weigh(1 - c)
-    s0[:, :half] = acc[...].astype(BF16)
-    s0[:, half:] = my_meta
     first_copy = remote(s0, r0, core_send.at[0], core_recv.at[0], partner)
     first_copy.start()
-    weigh(c)
+    acc[...] = weigh(c)
     first_copy.wait()
 
     def chip_piece(row):
@@ -185,15 +198,12 @@
     my_row = plane_peer(0)[1]
     chip_piece(my_row)
 
-    @pl.loop(0, tokens // 32, unroll=4)
+    @pl.loop(0, tokens // step, unroll=2)
     def _(i):
-        at = pl.ds(pl.multiple_of(i * 32, 32), 32)
+        at = pl.ds(pl.multiple_of(i * step, step), step)
         v = lbuf[at, :]
         ex = jnp.exp(v - jnp.max(v, axis=1, keepdims=True))
-        cbuf[at, :] = (ex / jnp.sum(ex, axis=1, keepdims=True)).astype(BF16)
-
-    comb_copy = pltpu.make_async_copy(cbuf, comb_hbm, csem.at[0])
-    comb_copy.start()
+        cbuf[at, :] = (ex * (1.0 / jnp.sum(ex, axis=1, keepdims=True))).astype(BF16)
 
     def merge(blocks):
         metas = [read_meta(b[:, half:]) for b in blocks]
@@ -281,15 +291,23 @@
     for copies in (plane_copies, column_copies, back_copies, gathers):
         for copy in copies.values():
             copy.wait_send()
-    comb_copy.wait()
-
-
-def mix_kernel(c_ref, g_ref, o_ref):
+
+
+def mix_kernel(c_ref, g_ref, o_hbm, obuf, sem):
     half = g_ref.shape[2]
-    for h in range(2):
-        o_ref[:, h * half:(h + 1) * half] = jnp.dot(
-            c_ref[...], g_ref[h], preferred_element_type=F32
-        ).astype(BF16)
+    blocks = sem.shape[0]
+    rows = obuf.shape[0] // blocks
+    copies = []
+    for i in range(blocks):
+        at = pl.ds(i * rows, rows)
+        for h in range(2):
+            obuf[at, h * half:(h + 1) * half] = jnp.dot(
+                c_ref[at, :], g_ref[h], preferred_element_type=F32
+            ).astype(BF16)
+        copies.append(pltpu.make_async_copy(obuf.at[at], o_hbm.at[at], sem.at[i]))
+        copies[-1].start()
+    for copy in copies:
+        copy.wait()
 
 
 def on_device(tokens, norm_gain, slot_param, w_in, w_out):
@@ -307,18 +325,21 @@
     combine, gathered = pl.pallas_call(
         moe_kernel,
         out_shape=(
-            jax.ShapeDtypeStruct((n, slots), BF16),
-            jax.ShapeDtypeStruct((2, slots, half), BF16),
+            pltpu.VMEM((n, slots), BF16),
+            pltpu.VMEM((2, slots, half), BF16),
         ),
-        in_specs=[anywhere, vmem, vmem, anywhere, anywhere],
-        out_specs=(anywhere, vmem),
+        in_specs=[anywhere] * 5,
+        out_specs=(vmem, vmem),
         scratch_shapes=[
             pltpu.VMEM((n, width), BF16),
+            pltpu.VMEM((n, width), BF16),
+            [pltpu.VMEM((n // chunks, width), BF16)] * 2,
             pltpu.VMEM((n, slots), F32),
-            pltpu.VMEM((n, slots), BF16),
             pltpu.VMEM((n, slots), BF16),
             pltpu.VMEM(w_in.shape, BF16),
             pltpu.VMEM(w_out.shape, BF16),
+            pltpu.VMEM((1, width), F32),
+            pltpu.VMEM((width, slots), BF16),
             pltpu.VMEM((8, slots), F32),
             pltpu.VMEM((slots, half), F32),
             pltpu.VMEM((slots, META), F32),
@@ -335,8 +356,7 @@
             pltpu.VMEM((group, half), BF16),
             pltpu.VMEM((COLUMN, piece, half), BF16),
             dma((chunks,)),
-            dma((2,)),
-            dma((1,)),
+            dma((4,)),
             dma((3,)), dma((3,)),
             dma((PLANE,)), dma((PLANE,)),
             dma((COLUMN,)), dma((COLUMN,)),
@@ -349,16 +369,14 @@
         ),
         name="moe",
     )(tokens, norm_gain.reshape(1, width), slot_param, w_in, w_out)
-    block = n // 8
+    blocks = 16
     return pl.pallas_call(
         mix_kernel,
-        grid=(8,),
         out_shape=jax.ShapeDtypeStruct((n, width), BF16),
-        in_specs=[
-            pl.BlockSpec((block, slots), lambda i: (i, 0)),
-            pl.BlockSpec((2, slots, half), lambda i: (0, 0, 0)),
-        ],
-        out_specs=pl.BlockSpec((block, width), lambda i: (i, 0)),
+        in_specs=[vmem, vmem],
+        out_specs=anywhere,
+        scratch_shapes=[pltpu.VMEM((n, width), BF16), dma((blocks,))],
+        compiler_params=pltpu.CompilerParams(vmem_limit_bytes=40 * 2**20),
         name="mix",
     )(combine, gathered)
 

time: 75.2 us -> 52.8 us (0.70)
  Pallas kernels: 71 us -> 50.8 us
  local copies, waits for them, and re-layouts: 3.84 us -> 1.73 us
    pallas_call x2, Pallas kernels: 71 us -> 50.8 us  [the longest x1 47.1 us: on_device(): pl.pallas_call(moe_kernel, out_shape=(pltpu.VMEM((n, slots), BF16), pltpu...]
    unnamed x8 -> x4, local copies, waits for them, and re-layouts: 3.84 us -> 1.73 us
where the time goes in v2:
time: 52.8 us; the launch traced here: 52.6 us
  Pallas kernels  50.8 us (96%)
  local copies, waits for them, and re-layouts  1.73 us (3%)
    pallas_call x1, Pallas kernels, on_device(): pl.pallas_call(moe_kernel, out_shape=(pltpu.VMEM((n, slots), BF16), pltpu...  47.1 us
    pallas_call x1, Pallas kernels, on_device(): pl.pallas_call(mix_kernel, out_shape=jax.ShapeDtypeStruct((n, width), BF1...  3.72 us
    unnamed x4, local copies, waits for them, and re-layouts  1.73 us

profile of v2, /device:TPU:1, one launch (start us, length us, event | category | flops | bytes accessed | tf_op | source)
XLA Modules:
  0.0 52.6 jit_solution(8014077338300454281)
XLA Ops:
  0.0 0.0 copy-start
  0.0 1.0 %copy-done = bf16[1024,256]{1,0:T(8,128)(2,1)S(1)} copy-done((bf16[1024,256]{1,0:T(8,128)(2,1)S(1)}, bf16[1024,256]{1,0:T(8,128)(2,1)}, u32[]{:S(2)}) %copy-start) | copy-done | bytes 524312
  1.0 0.0 copy-start.1
  1.0 0.7 %copy-done.1 = f32[1024]{0:T(1024)S(1)} copy-done((f32[1024]{0:T(1024)S(1)}, f32[1024]{0:T(1024)}, u32[]{:S(2)}) %copy-start.1) | copy-done | bytes 4120
  1.7 47.1 %moe.1 = (bf16[4096,256]{1,0:T(8,128)(2,1)S(1)}, bf16[2,256,512]{2,1,0:T(8,128)(2,1)S(1)}) custom-call(bf16[4096,1024]{1,0:T(8,128)(2,1)} %tok.1, f32[1,1024]{1,0:T(1,128)S(1)} %bitcast.1, bf16[1024,256]{1,0:T(8,128)(2,1)S(1)} %copy-done, bf16[8,1024,256]{2,1,0:T(8,128)(2,1)} %win_hbm.1, bf16[8,256,1024]{2,1,0:T(8,128)(2,1)} %wout_hbm.1), custom_call_target="tpu_custom_call" | custom-call | tf_op jit(solution)/shard_map/moe/pallas_call | solution.py:325
  48.9 3.7 %mix.1 = bf16[4096,1024]{1,0:T(8,128)(2,1)} custom-call(bf16[4096,256]{1,0:T(8,128)(2,1)S(1)} %get-tuple-element.7.c_ref, bf16[2,256,512]{2,1,0:T(8,128)(2,1)S(1)} %get-tuple-element.8.g_ref), custom_call_target="tpu_custom_call" | custom-call | tf_op jit(solution)/shard_map/mix/pallas_call | solution.py:373
Async XLA Ops:
  0.0 1.0 %copy-start = (bf16[1024,256]{1,0:T(8,128)(2,1)S(1)}, bf16[1024,256]{1,0:T(8,128)(2,1)}, u32[]{:S(2)}) copy-start(bf16[1024,256]{1,0:T(8,128)(2,1)} %slot_hbm.1) | copy-start | bytes 1572868
  1.0 0.7 %copy-start.1 = (f32[1024]{0:T(1024)S(1)}, f32[1024]{0:T(1024)}, u32[]{:S(2)}) copy-start(f32[1024]{0:T(1024)} %param.6) | copy-start | bytes 12292

commit v3 on v2

--- a/solution.py
+++ b/solution.py
@@ -11,7 +11,7 @@
 F32 = jnp.float32
 BF16 = jnp.bfloat16
 PLANE = 16
-COLUMN = 8
+COLUMN = 16
 META = 128
 
 
@@ -42,7 +42,7 @@
     tok, gain_hbm, slot_hbm, win_hbm, wout_hbm,
     cbuf, g_ref,
     raw, xbuf, pair, lbuf, dbuf, win, wout, gain_ref, slot_ref, mx, acc, colbuf,
-    s0, r0, s1, r1, s2, r2, sl, hbuf, xs, xr, s4, r4,
+    s0, r0, s1, r1, s2, r2, sl, hbuf, s4, r4,
     tsem, wsem,
     core_send, core_recv, plane_send, plane_recv, column_send, column_recv,
     back_send, back_recv, gather_send, gather_recv, fwd_send, fwd_recv,
@@ -79,8 +79,9 @@
         return (ps, pe), row
 
     def column_peer(k):
-        ps = ((bit(z1, k, 2) * 2 + bit(z0, k, 1)) * 2 + bit(xh, k, 0)) * 2 + c
-        return (ps, e)
+        ph, pc = bit(xh, k, 1), bit(c, k, 0)
+        ps = ((bit(z1, k, 3) * 2 + bit(z0, k, 2)) * 2 + ph) * 2 + pc
+        return (ps, e), pl.multiple_of(ph * piece, piece), pc
 
     partner = (s + 1 - 2 * c, e)
 
@@ -104,7 +105,7 @@
     barrier = pltpu.get_barrier_semaphore()
     greeted = [partner]
     greeted += [plane_peer(k)[0] for k in range(1, PLANE)]
-    greeted += [column_peer(k) for k in range(2, COLUMN)]
+    greeted += [column_peer(k)[0] for k in range(3, COLUMN)]
     for device in greeted:
         pl.semaphore_signal(barrier, inc=1, device_id=device, device_id_type=MESH)
     win_copy = pltpu.make_async_copy(win_hbm, win, wsem.at[0])
@@ -178,25 +179,22 @@
     acc[...] = weigh(c)
     first_copy.wait()
 
-    def chip_piece(row):
-        at = pl.ds(row, piece)
-        mine, my_total = colbuf[at, 0:1], colbuf[at, 1:2]
-        other, other_total = read_meta(r0[at, half:])
-        joint = jnp.maximum(mine, other)
-        wa, wb = jnp.exp(mine - joint), jnp.exp(other - joint)
-        s1[at, :half] = (acc[at, :] * wa + r0[at, :half].astype(F32) * wb).astype(BF16)
-        s1[at, half:] = meta_block(joint, my_total * wa + other_total * wb)
+    mine, my_total = colbuf[:, 0:1], colbuf[:, 1:2]
+    other, other_total = read_meta(r0[:, half:])
+    joint = jnp.maximum(mine, other)
+    wa, wb = jnp.exp(mine - joint), jnp.exp(other - joint)
+    s1[:, half:] = meta_block(joint, my_total * wa + other_total * wb)
+    s1[:, :half] = (acc[...] * wa + r0[:, :half].astype(F32) * wb).astype(BF16)
 
     order = sorted(range(1, PLANE), key=lambda k: -bin(k).count("1"))
     plane_copies = {}
     for k in order:
         device, row = plane_peer(k)
-        chip_piece(row)
-        at = pl.ds(row, piece)
-        plane_copies[k] = remote(s1.at[at], r1.at[k], plane_send.at[k], plane_recv.at[k], device)
+        plane_copies[k] = remote(
+            s1.at[pl.ds(row, piece)], r1.at[k], plane_send.at[k], plane_recv.at[k], device
+        )
         plane_copies[k].start()
     my_row = plane_peer(0)[1]
-    chip_piece(my_row)
 
     @pl.loop(0, tokens // step, unroll=2)
     def _(i):
@@ -218,22 +216,22 @@
     s2[:, :half] = summed.astype(BF16)
     s2[:, half:] = meta_block(joint, total_k)
 
+    column_order = sorted(range(1, COLUMN), key=lambda k: -bin(k).count("1"))
     column_copies = {}
-    for k in sorted(range(1, COLUMN), key=lambda k: -bin(k).count("1")):
-        column_copies[k] = remote(s2, r2.at[k], column_send.at[k], column_recv.at[k], column_peer(k))
+    for k in column_order:
+        column_copies[k] = remote(
+            s2, r2.at[k], column_send.at[k], column_recv.at[k], column_peer(k)[0]
+        )
         column_copies[k].start()
-    for k in range(1, COLUMN):
+    for k in column_order:
         column_copies[k].wait_recv()
-    for odd in range(2):
-        blocks = [s2[...] if k == 0 else r2[k] for k in range(odd, COLUMN, 2)]
+    for low in range(4):
+        blocks = [s2[...] if k == 0 else r2[k] for k in range(low, COLUMN, 4)]
         out, _, tot = merge(blocks)
-        at = pl.multiple_of((1 - xh if odd else xh) * piece, piece)
-        sl[c, pl.ds(at, piece), :] = (out / tot).astype(BF16)
-    in_copy = remote(sl.at[c], sl.at[c], core_send.at[1], core_recv.at[1], partner)
-    in_copy.start()
+        _, at, there = column_peer(low)
+        sl[there, pl.ds(at, piece), :] = (out / tot).astype(BF16)
     win_copy.wait()
     wout_copy.wait()
-    in_copy.wait()
 
     owner = lax.broadcasted_iota(jnp.int32, (group, hidden), 0) // per
     first = jnp.zeros((group, hidden), F32)
@@ -246,27 +244,25 @@
         hbuf[:, x * hidden:(x + 1) * hidden] = jnp.where(owner == x, act, 0.0).astype(BF16)
 
     def project(h):
-        cols = pl.ds(pl.multiple_of(h * half, half), half)
+        cols = slice(h * half, (h + 1) * half)
         return sum(
             jnp.dot(hbuf[:, x * hidden:(x + 1) * hidden], wout[x, :, cols], preferred_element_type=F32)
             for x in range(local_experts)
         )
 
-    xs[...] = project(1 - c).astype(BF16)
-    out_copy = remote(xs, xr, core_send.at[2], core_recv.at[2], partner)
-    out_copy.start()
-    own = project(c)
-    out_copy.wait()
-    s4[...] = (own + xr[...].astype(F32)).astype(BF16)
-
+    s4[0] = project(0).astype(BF16)
+    s4[1] = project(1).astype(BF16)
     back_copies = {}
-    for k in sorted(range(1, COLUMN), key=lambda k: -bin(k).count("1")):
-        at = pl.ds(pl.multiple_of(bit(xh, k, 0) * piece, piece), piece)
-        back_copies[k] = remote(s4.at[at], r4.at[k], back_send.at[k], back_recv.at[k], column_peer(k))
+    for k in column_order:
+        device, at, there = column_peer(k)
+        back_copies[k] = remote(
+            s4.at[there, pl.ds(at, piece)], r4.at[k], back_send.at[k], back_recv.at[k], device
+        )
         back_copies[k].start()
-    mine = s4[pl.ds(pl.multiple_of(xh * piece, piece), piece), :].astype(F32)
-    for k in range(1, COLUMN):
+    mine = s4[c, pl.ds(column_peer(0)[1], piece), :].astype(F32)
+    for k in column_order:
         back_copies[k].wait_recv()
+    for k in column_order:
         mine += r4[k].astype(F32)
     at = pl.ds(my_row, piece)
     g_ref[c, at, :] = mine.astype(BF16)
@@ -320,7 +316,7 @@
     chunks = 8
     wide = half + META
     dma = pltpu.SemaphoreType.DMA
-    anywhere = pl.BlockSpec(memory_space=pl.ANY)
+    anywhere = pl.BlockSpec(memory_space=pltpu.HBM)
     vmem = pl.BlockSpec(memory_space=pltpu.VMEM)
     combine, gathered = pl.pallas_call(
         moe_kernel,
@@ -351,13 +347,11 @@
             pltpu.VMEM((COLUMN, piece, wide), BF16),
             pltpu.VMEM((2, group, half), BF16),
             pltpu.VMEM((group, w_in.shape[0] * hidden), BF16),
-            pltpu.VMEM((group, half), BF16),
-            pltpu.VMEM((group, half), BF16),
-            pltpu.VMEM((group, half), BF16),
+            pltpu.VMEM((2, group, half), BF16),
             pltpu.VMEM((COLUMN, piece, half), BF16),
             dma((chunks,)),
             dma((4,)),
-            dma((3,)), dma((3,)),
+            dma((1,)), dma((1,)),
             dma((PLANE,)), dma((PLANE,)),
             dma((COLUMN,)), dma((COLUMN,)),
             dma((COLUMN,)), dma((COLUMN,)),
@@ -368,7 +362,12 @@
             collective_id=0, has_side_effects=True, vmem_limit_bytes=48 * 2**20
         ),
         name="moe",
-    )(tokens, norm_gain.reshape(1, width), slot_param, w_in, w_out)
+    )(
+        *(
+            pltpu.with_memory_space_constraint(a, pltpu.HBM)
+            for a in (tokens, norm_gain.reshape(1, width), slot_param, w_in, w_out)
+        )
+    )
     blocks = 16
     return pl.pallas_call(
         mix_kernel,

time: 52.8 us -> 52.4 us (level)
  local copies, waits for them, and re-layouts: 1.73 us -> 0 us
  Pallas kernels: 50.8 us -> 52.3 us
    unnamed x4 -> x0, local copies, waits for them, and re-layouts: 1.73 us -> none
    pallas_call x1, Pallas kernels: 47.1 us -> 48.6 us  [on_device(): pl.pallas_call(moe_kernel, out_shape=(pltpu.VMEM((n, slots), BF16), pltpu...]
where the time goes in v3:
time: 52.4 us; the launch traced here: 52.3 us
  Pallas kernels  52.3 us (100%)
    pallas_call x1, Pallas kernels, on_device(): pl.pallas_call(moe_kernel, out_shape=(pltpu.VMEM((n, slots), BF16), pltpu...  48.6 us
    pallas_call x1, Pallas kernels, on_device(): pl.pallas_call(mix_kernel, out_shape=jax.ShapeDtypeStruct((n, width), BF1...  3.72 us

profile of v3, /device:TPU:1, one launch (start us, length us, event | category | flops | bytes accessed | tf_op | source)
XLA Modules:
  0.0 52.3 jit_solution(266851069664769378)
XLA Ops:
  0.0 48.6 %moe.1 = (bf16[4096,256]{1,0:T(8,128)(2,1)S(1)}, bf16[2,256,512]{2,1,0:T(8,128)(2,1)S(1)}) custom-call(bf16[4096,1024]{1,0:T(8,128)(2,1)} %tok.1, f32[1,1024]{1,0:T(1,128)} %bitcast.1, bf16[1024,256]{1,0:T(8,128)(2,1)} %slot_hbm.1, bf16[8,1024,256]{2,1,0:T(8,128)(2,1)} %win_hbm.1, bf16[8,256,1024]{2,1,0:T(8,128)(2,1)} %wout_hbm.1), custom_call_target="tpu_custom_call" | custom-call | tf_op jit(solution)/shard_map/moe/pallas_call | solution.py:321
  48.6 3.7 %mix.1 = bf16[4096,1024]{1,0:T(8,128)(2,1)} custom-call(bf16[4096,256]{1,0:T(8,128)(2,1)S(1)} %get-tuple-element.7.c_ref, bf16[2,256,512]{2,1,0:T(8,128)(2,1)S(1)} %get-tuple-element.8.g_ref), custom_call_target="tpu_custom_call" | custom-call | tf_op jit(solution)/shard_map/mix/pallas_call | solution.py:372

commit v4 on v3

--- a/solution.py
+++ b/solution.py
@@ -11,7 +11,7 @@
 F32 = jnp.float32
 BF16 = jnp.bfloat16
 PLANE = 16
-COLUMN = 16
+COLUMN = 8
 META = 128
 
 
@@ -40,9 +40,9 @@
 
 def moe_kernel(
     tok, gain_hbm, slot_hbm, win_hbm, wout_hbm,
-    cbuf, g_ref,
+    cbuf, g_ref, begun,
     raw, xbuf, pair, lbuf, dbuf, win, wout, gain_ref, slot_ref, mx, acc, colbuf,
-    s0, r0, s1, r1, s2, r2, sl, hbuf, s4, r4,
+    s0, r0, s1, r1, s2, r2, sl, hbuf, xs, xr, s4, r4,
     tsem, wsem,
     core_send, core_recv, plane_send, plane_recv, column_send, column_recv,
     back_send, back_recv, gather_send, gather_recv, fwd_send, fwd_recv,
@@ -79,9 +79,9 @@
         return (ps, pe), row
 
     def column_peer(k):
-        ph, pc = bit(xh, k, 1), bit(c, k, 0)
-        ps = ((bit(z1, k, 3) * 2 + bit(z0, k, 2)) * 2 + ph) * 2 + pc
-        return (ps, e), pl.multiple_of(ph * piece, piece), pc
+        ph = bit(xh, k, 0)
+        ps = ((bit(z1, k, 2) * 2 + bit(z0, k, 1)) * 2 + ph) * 2 + c
+        return (ps, e), pl.multiple_of(ph * piece, piece)
 
     partner = (s + 1 - 2 * c, e)
 
@@ -105,7 +105,7 @@
     barrier = pltpu.get_barrier_semaphore()
     greeted = [partner]
     greeted += [plane_peer(k)[0] for k in range(1, PLANE)]
-    greeted += [column_peer(k)[0] for k in range(3, COLUMN)]
+    greeted += [column_peer(k)[0] for k in range(2, COLUMN)]
     for device in greeted:
         pl.semaphore_signal(barrier, inc=1, device_id=device, device_id_type=MESH)
     win_copy = pltpu.make_async_copy(win_hbm, win, wsem.at[0])
@@ -225,41 +225,51 @@
         column_copies[k].start()
     for k in column_order:
         column_copies[k].wait_recv()
-    for low in range(4):
-        blocks = [s2[...] if k == 0 else r2[k] for k in range(low, COLUMN, 4)]
-        out, _, tot = merge(blocks)
-        _, at, there = column_peer(low)
-        sl[there, pl.ds(at, piece), :] = (out / tot).astype(BF16)
+    for low in range(2):
+        out, _, tot = merge([s2[...] if k == 0 else r2[k] for k in range(low, COLUMN, 2)])
+        sl[c, pl.ds(column_peer(low)[1], piece), :] = (out / tot).astype(BF16)
+    in_copy = remote(sl.at[c], sl.at[c], core_send.at[1], core_recv.at[1], partner)
+    in_copy.start()
     win_copy.wait()
     wout_copy.wait()
 
     owner = lax.broadcasted_iota(jnp.int32, (group, hidden), 0) // per
-    first = jnp.zeros((group, hidden), F32)
-    for x in range(local_experts):
-        y = jnp.dot(sl[0], win[x, :half, :], preferred_element_type=F32)
-        y += jnp.dot(sl[1], win[x, half:, :], preferred_element_type=F32)
-        first = jnp.where(owner == x, y, first)
+
+    def enter(h, first):
+        rows_in = pl.ds(pl.multiple_of(h * half, half), half)
+        for x in range(local_experts):
+            y = jnp.dot(sl[h], win[x, rows_in, :], preferred_element_type=F32)
+            first = jnp.where(owner == x, first + y, first)
+        return first
+
+    first = enter(c, jnp.zeros((group, hidden), F32))
+    in_copy.wait()
+    first = enter(1 - c, first)
     act = 0.5 * first * (1.0 + lax.erf(first * 0.7071067811865476))
     for x in range(local_experts):
         hbuf[:, x * hidden:(x + 1) * hidden] = jnp.where(owner == x, act, 0.0).astype(BF16)
 
     def project(h):
-        cols = slice(h * half, (h + 1) * half)
+        cols = pl.ds(pl.multiple_of(h * half, half), half)
         return sum(
             jnp.dot(hbuf[:, x * hidden:(x + 1) * hidden], wout[x, :, cols], preferred_element_type=F32)
             for x in range(local_experts)
         )
 
-    s4[0] = project(0).astype(BF16)
-    s4[1] = project(1).astype(BF16)
+    xs[...] = project(1 - c).astype(BF16)
+    out_copy = remote(xs, xr, core_send.at[2], core_recv.at[2], partner)
+    out_copy.start()
+    own = project(c)
+    out_copy.wait()
+    s4[...] = (own + xr[...].astype(F32)).astype(BF16)
     back_copies = {}
     for k in column_order:
-        device, at, there = column_peer(k)
+        device, at = column_peer(k)
         back_copies[k] = remote(
-            s4.at[there, pl.ds(at, piece)], r4.at[k], back_send.at[k], back_recv.at[k], device
+            s4.at[pl.ds(at, piece)], r4.at[k], back_send.at[k], back_recv.at[k], device
         )
         back_copies[k].start()
-    mine = s4[c, pl.ds(column_peer(0)[1], piece), :].astype(F32)
+    mine = s4[pl.ds(column_peer(0)[1], piece), :].astype(F32)
     for k in column_order:
         back_copies[k].wait_recv()
     for k in column_order:
@@ -282,6 +292,11 @@
             remote(g_ref.at[c, there], g_ref.at[c, there], fwd_send.at[k], fwd_recv.at[k], partner)
         )
         forwards[-1].start()
+    for i in range(4):
+        at = pl.ds(i * (tokens // 4), tokens // 4)
+        begun[at, :] = jnp.dot(
+            cbuf[at, :], g_ref[c], preferred_element_type=F32
+        ).astype(BF16)
     for copy in forwards:
         copy.wait()
     for copies in (plane_copies, column_copies, back_copies, gathers):
@@ -289,18 +304,21 @@
             copy.wait_send()
 
 
-def mix_kernel(c_ref, g_ref, o_hbm, obuf, sem):
+def mix_kernel(c_ref, g_ref, begun, o_hbm, obuf, sem, begun_sem):
     half = g_ref.shape[2]
     blocks = sem.shape[0]
     rows = obuf.shape[0] // blocks
-    copies = []
+    c = lax.rem(lax.axis_index("seq"), 2)
+    mine = pl.ds(pl.multiple_of(c * half, half), half)
+    rest = pl.ds(pl.multiple_of((1 - c) * half, half), half)
+    copies = [pltpu.make_async_copy(begun, o_hbm.at[:, mine], begun_sem.at[0])]
+    copies[0].start()
     for i in range(blocks):
         at = pl.ds(i * rows, rows)
-        for h in range(2):
-            obuf[at, h * half:(h + 1) * half] = jnp.dot(
-                c_ref[at, :], g_ref[h], preferred_element_type=F32
-            ).astype(BF16)
-        copies.append(pltpu.make_async_copy(obuf.at[at], o_hbm.at[at], sem.at[i]))
+        obuf[at, :] = jnp.dot(
+            c_ref[at, :], g_ref[1 - c], preferred_element_type=F32
+        ).astype(BF16)
+        copies.append(pltpu.make_async_copy(obuf.at[at], o_hbm.at[at, rest], sem.at[i]))
         copies[-1].start()
     for copy in copies:
         copy.wait()
@@ -318,14 +336,15 @@
     dma = pltpu.SemaphoreType.DMA
     anywhere = pl.BlockSpec(memory_space=pltpu.HBM)
     vmem = pl.BlockSpec(memory_space=pltpu.VMEM)
-    combine, gathered = pl.pallas_call(
+    combine, gathered, begun = pl.pallas_call(
         moe_kernel,
         out_shape=(
             pltpu.VMEM((n, slots), BF16),
             pltpu.VMEM((2, slots, half), BF16),
+            pltpu.VMEM((n, half), BF16),
         ),
         in_specs=[anywhere] * 5,
-        out_specs=(vmem, vmem),
+        out_specs=(vmem, vmem, vmem),
         scratch_shapes=[
             pltpu.VMEM((n, width), BF16),
             pltpu.VMEM((n, width), BF16),
@@ -347,11 +366,13 @@
             pltpu.VMEM((COLUMN, piece, wide), BF16),
             pltpu.VMEM((2, group, half), BF16),
             pltpu.VMEM((group, w_in.shape[0] * hidden), BF16),
-            pltpu.VMEM((2, group, half), BF16),
+            pltpu.VMEM((group, half), BF16),
+            pltpu.VMEM((group, half), BF16),
+            pltpu.VMEM((group, half), BF16),
             pltpu.VMEM((COLUMN, piece, half), BF16),
             dma((chunks,)),
             dma((4,)),
-            dma((1,)), dma((1,)),
+            dma((3,)), dma((3,)),
             dma((PLANE,)), dma((PLANE,)),
             dma((COLUMN,)), dma((COLUMN,)),
             dma((COLUMN,)), dma((COLUMN,)),
@@ -368,16 +389,15 @@
             for a in (tokens, norm_gain.reshape(1, width), slot_param, w_in, w_out)
         )
     )
-    blocks = 16
     return pl.pallas_call(
         mix_kernel,
         out_shape=jax.ShapeDtypeStruct((n, width), BF16),
-        in_specs=[vmem, vmem],
+        in_specs=[vmem, vmem, vmem],
         out_specs=anywhere,
-        scratch_shapes=[pltpu.VMEM((n, width), BF16), dma((blocks,))],
+        scratch_shapes=[pltpu.VMEM((n, half), BF16), dma((8,)), dma((1,))],
         compiler_params=pltpu.CompilerParams(vmem_limit_bytes=40 * 2**20),
         name="mix",
-    )(combine, gathered)
+    )(combine, gathered, begun)
 
 
 def solution(mesh):

time: 52.4 us -> 50.8 us (0.969)
  Pallas kernels: 52.3 us -> 50.7 us
    pallas_call x1, Pallas kernels: 48.6 us -> 47.3 us  [on_device(): pl.pallas_call(moe_kernel, out_shape=(pltpu.VMEM((n, slots), BF16), pltpu...]
where the time goes in v4:
time: 50.8 us; the launch traced here: 50.7 us
  Pallas kernels  50.7 us (100%)
    pallas_call x1, Pallas kernels, on_device(): pl.pallas_call(moe_kernel, out_shape=(pltpu.VMEM((n, slots), BF16), pltpu...  47.3 us
    pallas_call x1, Pallas kernels, on_device(): pl.pallas_call(mix_kernel, out_shape=jax.ShapeDtypeStruct((n, width), BF1...  3.38 us

profile of v4, /device:TPU:1, one launch (start us, length us, event | category | flops | bytes accessed | tf_op | source)
XLA Modules:
  0.0 50.7 jit_solution(17004585876001950058)
XLA Ops:
  0.0 47.3 %moe.1 = (bf16[4096,256]{1,0:T(8,128)(2,1)S(1)}, bf16[2,256,512]{2,1,0:T(8,128)(2,1)S(1)}, bf16[4096,512]{1,0:T(8,128)(2,1)S(1)}) custom-call(bf16[4096,1024]{1,0:T(8,128)(2,1)} %tok.1, f32[1,1024]{1,0:T(1,128)} %bitcast.1, bf16[1024,256]{1,0:T(8,128)(2,1)} %slot_hbm.1, bf16[8,1024,256]{2,1,0:T(8,128)(2,1)} %win_hbm.1, bf16[8,256,1024]{2,1,0:T(8,128)(2,1)} %wout_hbm.1), custom_call_target="tpu_custom_call" | custom-call | tf_op jit(solution)/shard_map/moe/pallas_call | solution.py:339
  47.3 3.4 %mix.1 = bf16[4096,1024]{1,0:T(8,128)(2,1)} custom-call(bf16[4096,256]{1,0:T(8,128)(2,1)S(1)} %get-tuple-element.8.c_ref, bf16[2,256,512]{2,1,0:T(8,128)(2,1)S(1)} %get-tuple-element.9.g_ref, bf16[4096,512]{1,0:T(8,128)(2,1)S(1)} %get-tuple-element.10.begun), custom_call_target="tpu_custom_call" | custom-call | tf_op jit(solution)/shard_map/mix/pallas_call | solution.py:392

commit v5 on v4

--- a/solution.py
+++ b/solution.py
@@ -95,10 +95,10 @@
         at = pl.ds(pl.multiple_of(i * rows, rows), rows)
         return pltpu.make_async_copy(tok.at[at], raw.at[at], tsem.at[i])
 
-    token_copy(0).start()
     gain_copy = pltpu.make_async_copy(gain_hbm, gain_ref, wsem.at[2])
     slot_copy = pltpu.make_async_copy(slot_hbm, slot_ref, wsem.at[3])
     gain_copy.start()
+    token_copy(0).start()
     slot_copy.start()
     for i in range(1, chunks):
         token_copy(i).start()
@@ -112,7 +112,6 @@
     wout_copy = pltpu.make_async_copy(wout_hbm, wout, wsem.at[1])
 
     gain_copy.wait()
-    slot_copy.wait()
     gain = gain_ref[...]
     mx[...] = jnp.full(mx.shape, -jnp.inf, F32)
 
@@ -133,11 +132,13 @@
 
     token_copy(0).wait()
     norm(0, 0)
+    slot_copy.wait()
 
     @pl.loop(0, chunks // 2 - 1)
     def _(i):
+        token_copy(2 * i + 1).wait()
+        token_copy(2 * i + 2).wait()
         for slot in range(2):
-            token_copy(2 * i + slot + 1).wait()
             norm(2 * i + slot + 1, 1 - slot)
             project_slots(2 * i + slot, slot)
 
@@ -292,8 +293,9 @@
             remote(g_ref.at[c, there], g_ref.at[c, there], fwd_send.at[k], fwd_recv.at[k], partner)
         )
         forwards[-1].start()
-    for i in range(4):
-        at = pl.ds(i * (tokens // 4), tokens // 4)
+    early = begun.shape[0] // 2
+    for i in range(2):
+        at = pl.ds(i * early, early)
         begun[at, :] = jnp.dot(
             cbuf[at, :], g_ref[c], preferred_element_type=F32
         ).astype(BF16)
@@ -306,19 +308,20 @@
 
 def mix_kernel(c_ref, g_ref, begun, o_hbm, obuf, sem, begun_sem):
     half = g_ref.shape[2]
-    blocks = sem.shape[0]
-    rows = obuf.shape[0] // blocks
+    rows = obuf.shape[1]
+    blocks = o_hbm.shape[0] // rows
     c = lax.rem(lax.axis_index("seq"), 2)
     mine = pl.ds(pl.multiple_of(c * half, half), half)
     rest = pl.ds(pl.multiple_of((1 - c) * half, half), half)
-    copies = [pltpu.make_async_copy(begun, o_hbm.at[:, mine], begun_sem.at[0])]
+    early = begun.shape[0]
+    copies = [pltpu.make_async_copy(begun, o_hbm.at[pl.ds(0, early), mine], begun_sem.at[0])]
     copies[0].start()
-    for i in range(blocks):
-        at = pl.ds(i * rows, rows)
-        obuf[at, :] = jnp.dot(
-            c_ref[at, :], g_ref[1 - c], preferred_element_type=F32
-        ).astype(BF16)
-        copies.append(pltpu.make_async_copy(obuf.at[at], o_hbm.at[at, rest], sem.at[i]))
+    todo = [(i * rows, 1 - c, rest) for i in range(blocks)]
+    todo += [(i * rows, c, mine) for i in range(early // rows, blocks)]
+    for i, (row, h, cols) in enumerate(todo):
+        at = pl.ds(row, rows)
+        obuf[i] = jnp.dot(c_ref[at, :], g_ref[h], preferred_element_type=F32).astype(BF16)
+        copies.append(pltpu.make_async_copy(obuf.at[i], o_hbm.at[at, cols], sem.at[i]))
         copies[-1].start()
     for copy in copies:
         copy.wait()
@@ -331,7 +334,7 @@
     group = slots // lax.axis_size("exp")
     piece = group // 2
     hidden = w_in.shape[2]
-    chunks = 8
+    chunks = 16
     wide = half + META
     dma = pltpu.SemaphoreType.DMA
     anywhere = pl.BlockSpec(memory_space=pltpu.HBM)
@@ -341,7 +344,7 @@
         out_shape=(
             pltpu.VMEM((n, slots), BF16),
             pltpu.VMEM((2, slots, half), BF16),
-            pltpu.VMEM((n, half), BF16),
+            pltpu.VMEM((n // 2, half), BF16),
         ),
         in_specs=[anywhere] * 5,
         out_specs=(vmem, vmem, vmem),
@@ -394,7 +397,7 @@
         out_shape=jax.ShapeDtypeStruct((n, width), BF16),
         in_specs=[vmem, vmem, vmem],
         out_specs=anywhere,
-        scratch_shapes=[pltpu.VMEM((n, half), BF16), dma((8,)), dma((1,))],
+        scratch_shapes=[pltpu.VMEM((12, n // 8, half), BF16), dma((12,)), dma((1,))],
         compiler_params=pltpu.CompilerParams(vmem_limit_bytes=40 * 2**20),
         name="mix",
     )(combine, gathered, begun)

time: 50.8 us -> 49.1 us (0.967)
  Pallas kernels: 50.7 us -> 48.9 us
    pallas_call x1, Pallas kernels: 47.3 us -> 45.5 us  [on_device(): pl.pallas_call(moe_kernel, out_shape=(pltpu.VMEM((n, slots), BF16), pltpu...]
where the time goes in v5:
time: 49.1 us; the launch traced here: 49 us
  Pallas kernels  48.9 us (100%)
    pallas_call x1, Pallas kernels, on_device(): pl.pallas_call(moe_kernel, out_shape=(pltpu.VMEM((n, slots), BF16), pltpu...  45.5 us
    pallas_call x1, Pallas kernels, on_device(): pl.pallas_call(mix_kernel, out_shape=jax.ShapeDtypeStruct((n, width), BF1...  3.41 us

profile of v5, /device:TPU:1, one launch (start us, length us, event | category | flops | bytes accessed | tf_op | source)
XLA Modules:
  0.0 49.0 jit_solution(14925974470845103430)
XLA Ops:
  0.0 45.5 %moe.1 = (bf16[4096,256]{1,0:T(8,128)(2,1)S(1)}, bf16[2,256,512]{2,1,0:T(8,128)(2,1)S(1)}, bf16[2048,512]{1,0:T(8,128)(2,1)S(1)}) custom-call(bf16[4096,1024]{1,0:T(8,128)(2,1)} %tok.1, f32[1,1024]{1,0:T(1,128)} %bitcast.1, bf16[1024,256]{1,0:T(8,128)(2,1)} %slot_hbm.1, bf16[8,1024,256]{2,1,0:T(8,128)(2,1)} %win_hbm.1, bf16[8,256,1024]{2,1,0:T(8,128)(2,1)} %wout_hbm.1), custom_call_target="tpu_custom_call" | custom-call | tf_op jit(solution)/shard_map/moe/pallas_call | solution.py:342
  45.5 3.4 %mix.1 = bf16[4096,1024]{1,0:T(8,128)(2,1)} custom-call(bf16[4096,256]{1,0:T(8,128)(2,1)S(1)} %get-tuple-element.8.c_ref, bf16[2,256,512]{2,1,0:T(8,128)(2,1)S(1)} %get-tuple-element.9.g_ref, bf16[2048,512]{1,0:T(8,128)(2,1)S(1)} %get-tuple-element.10.begun), custom_call_target="tpu_custom_call" | custom-call | tf_op jit(solution)/shard_map/mix/pallas_call | solution.py:395

commit v6 on v5

--- a/solution.py
+++ b/solution.py
@@ -13,6 +13,17 @@
 PLANE = 16
 COLUMN = 8
 META = 128
+
+
+RING = (0, 1, 2, 1)
+
+
+def plane_hops(k):
+    return RING[(k >> 3 & 1) * 2 + (k & 1)] + RING[k >> 1 & 3]
+
+
+def column_hops(k):
+    return RING[(k & 1) * 2] + RING[k >> 1 & 3]
 
 
 def split3(v):
@@ -143,23 +154,23 @@
             project_slots(2 * i + slot, slot)
 
     token_copy(chunks - 1).wait()
+    win_copy.start()
+    wout_copy.start()
     norm(chunks - 1, 1)
     project_slots(chunks - 2, 0)
     project_slots(chunks - 1, 1)
 
-    win_copy.start()
-    wout_copy.start()
     peak = jnp.max(mx[...], axis=0, keepdims=True)
 
     step = min(256, tokens)
 
-    def dispatch(i, total):
-        at = pl.ds(pl.multiple_of(i * step, step), step)
+    total = jnp.zeros((8, slots), F32)
+    for i in range(tokens // step):
+        at = pl.ds(i * step, step)
         ex = jnp.exp(lbuf[at, :] - peak)
         dbuf[at, :] = ex.astype(BF16)
-        return total + jnp.sum(ex.reshape(step // 8, 8, slots), axis=0)
-
-    total = lax.fori_loop(0, tokens // step, dispatch, jnp.zeros((8, slots), F32))
+        total += jnp.sum(ex.reshape(step // 8, 8, slots), axis=0)
+
     total = jnp.sum(total, axis=0, keepdims=True)
     line = lax.broadcasted_iota(jnp.int32, (META, slots), 0)
     both = jnp.where(line == 0, peak, jnp.where(line == 1, total, 0.0))
@@ -187,7 +198,7 @@
     s1[:, half:] = meta_block(joint, my_total * wa + other_total * wb)
     s1[:, :half] = (acc[...] * wa + r0[:, :half].astype(F32) * wb).astype(BF16)
 
-    order = sorted(range(1, PLANE), key=lambda k: -bin(k).count("1"))
+    order = sorted(range(1, PLANE), key=plane_hops, reverse=True)
     plane_copies = {}
     for k in order:
         device, row = plane_peer(k)
@@ -217,7 +228,7 @@
     s2[:, :half] = summed.astype(BF16)
     s2[:, half:] = meta_block(joint, total_k)
 
-    column_order = sorted(range(1, COLUMN), key=lambda k: -bin(k).count("1"))
+    column_order = sorted(range(1, COLUMN), key=column_hops, reverse=True)
     column_copies = {}
     for k in column_order:
         column_copies[k] = remote(

time: 49.1 us -> 48.3 us (0.984)
  Pallas kernels: 48.9 us -> 48.2 us
    pallas_call x1, Pallas kernels: 45.5 us -> 44.8 us  [on_device(): pl.pallas_call(moe_kernel, out_shape=(pltpu.VMEM((n, slots), BF16), pltpu...]
where the time goes in v6:
time: 48.3 us; the launch traced here: 48.2 us
  Pallas kernels  48.2 us (100%)
    pallas_call x1, Pallas kernels, on_device(): pl.pallas_call(moe_kernel, out_shape=(pltpu.VMEM((n, slots), BF16), pltpu...  44.8 us
    pallas_call x1, Pallas kernels, on_device(): pl.pallas_call(mix_kernel, out_shape=jax.ShapeDtypeStruct((n, width), BF1...  3.41 us

profile of v6, /device:TPU:1, one launch (start us, length us, event | category | flops | bytes accessed | tf_op | source)
XLA Modules:
  0.0 48.2 jit_solution(1788306854840455639)
XLA Ops:
  0.0 44.8 %moe.1 = (bf16[4096,256]{1,0:T(8,128)(2,1)S(1)}, bf16[2,256,512]{2,1,0:T(8,128)(2,1)S(1)}, bf16[2048,512]{1,0:T(8,128)(2,1)S(1)}) custom-call(bf16[4096,1024]{1,0:T(8,128)(2,1)} %tok.1, f32[1,1024]{1,0:T(1,128)} %bitcast.1, bf16[1024,256]{1,0:T(8,128)(2,1)} %slot_hbm.1, bf16[8,1024,256]{2,1,0:T(8,128)(2,1)} %win_hbm.1, bf16[8,256,1024]{2,1,0:T(8,128)(2,1)} %wout_hbm.1), custom_call_target="tpu_custom_call" | custom-call | tf_op jit(solution)/shard_map/moe/pallas_call | solution.py:353
  44.8 3.4 %mix.1 = bf16[4096,1024]{1,0:T(8,128)(2,1)} custom-call(bf16[4096,256]{1,0:T(8,128)(2,1)S(1)} %get-tuple-element.8.c_ref, bf16[2,256,512]{2,1,0:T(8,128)(2,1)S(1)} %get-tuple-element.9.g_ref, bf16[2048,512]{1,0:T(8,128)(2,1)S(1)} %get-tuple-element.10.begun), custom_call_target="tpu_custom_call" | custom-call | tf_op jit(solution)/shard_map/mix/pallas_call | solution.py:406

commit v7 on v6

--- a/solution.py
+++ b/solution.py
@@ -13,6 +13,7 @@
 PLANE = 16
 COLUMN = 8
 META = 128
+EARLY = 5
 
 
 RING = (0, 1, 2, 1)
@@ -111,7 +112,7 @@
     gain_copy.start()
     token_copy(0).start()
     slot_copy.start()
-    for i in range(1, chunks):
+    for i in range(1, EARLY):
         token_copy(i).start()
     barrier = pltpu.get_barrier_semaphore()
     greeted = [partner]
@@ -142,6 +143,8 @@
         mx[...] = jnp.maximum(mx[...], jnp.max(logits.reshape(rows // 8, 8, slots), axis=0))
 
     token_copy(0).wait()
+    for i in range(EARLY, chunks):
+        token_copy(i).start()
     norm(0, 0)
     slot_copy.wait()
 

time: 48.3 us -> 46.6 us (0.965)
  Pallas kernels: 48.2 us -> 46.5 us
    pallas_call x1, Pallas kernels: 44.8 us -> 43.1 us  [on_device(): pl.pallas_call(moe_kernel, out_shape=(pltpu.VMEM((n, slots), BF16), pltpu...]
where the time goes in v7:
time: 46.6 us; the launch traced here: 46.5 us
  Pallas kernels  46.5 us (100%)
    pallas_call x1, Pallas kernels, on_device(): pl.pallas_call(moe_kernel, out_shape=(pltpu.VMEM((n, slots), BF16), pltpu...  43.1 us
    pallas_call x1, Pallas kernels, on_device(): pl.pallas_call(mix_kernel, out_shape=jax.ShapeDtypeStruct((n, width), BF1...  3.41 us

profile of v7, /device:TPU:1, one launch (start us, length us, event | category | flops | bytes accessed | tf_op | source)
XLA Modules:
  0.0 46.5 jit_solution(620702838118510827)
XLA Ops:
  0.0 43.1 %moe.1 = (bf16[4096,256]{1,0:T(8,128)(2,1)S(1)}, bf16[2,256,512]{2,1,0:T(8,128)(2,1)S(1)}, bf16[2048,512]{1,0:T(8,128)(2,1)S(1)}) custom-call(bf16[4096,1024]{1,0:T(8,128)(2,1)} %tok.1, f32[1,1024]{1,0:T(1,128)} %bitcast.1, bf16[1024,256]{1,0:T(8,128)(2,1)} %slot_hbm.1, bf16[8,1024,256]{2,1,0:T(8,128)(2,1)} %win_hbm.1, bf16[8,256,1024]{2,1,0:T(8,128)(2,1)} %wout_hbm.1), custom_call_target="tpu_custom_call" | custom-call | tf_op jit(solution)/shard_map/moe/pallas_call | solution.py:356
  43.1 3.4 %mix.1 = bf16[4096,1024]{1,0:T(8,128)(2,1)} custom-call(bf16[4096,256]{1,0:T(8,128)(2,1)S(1)} %get-tuple-element.8.c_ref, bf16[2,256,512]{2,1,0:T(8,128)(2,1)S(1)} %get-tuple-element.9.g_ref, bf16[2048,512]{1,0:T(8,128)(2,1)S(1)} %get-tuple-element.10.begun), custom_call_target="tpu_custom_call" | custom-call | tf_op jit(solution)/shard_map/mix/pallas_call | solution.py:409

commit v8 on v7

--- a/solution.py
+++ b/solution.py
@@ -35,19 +35,23 @@
 
 
 def meta_block(peak, total):
-    rows = peak.shape[0]
-    lane = lax.broadcasted_iota(jnp.int32, (rows, META), 1)
-    out = jnp.zeros((rows, META), F32)
+    lane = lax.broadcasted_iota(jnp.int32, peak.shape, 1)
+    out = jnp.zeros(peak.shape, F32)
     for i, part in enumerate(split3(peak) + split3(total)):
         out = jnp.where(lane == i, part, out)
     return out.astype(BF16)
 
 
 def read_meta(block):
-    v = block.astype(F32)
-    peak = v[:, 0:1] + v[:, 1:2] + v[:, 2:3]
-    total = v[:, 3:4] + v[:, 4:5] + v[:, 5:6]
-    return peak, total
+    row = lax.broadcasted_iota(jnp.int32, (META, 2 * META), 0) // 3
+    column = lax.broadcasted_iota(jnp.int32, (META, 2 * META), 1) // META
+    pick = jnp.where(row == column, 1.0, 0.0).astype(BF16)
+    both = jnp.dot(block, pick, preferred_element_type=F32)
+    return both[:, :META], both[:, META:]
+
+
+def wide(v, width):
+    return jnp.concatenate([v] * (width // META), axis=1)
 
 
 def moe_kernel(
@@ -175,10 +179,9 @@
         total += jnp.sum(ex.reshape(step // 8, 8, slots), axis=0)
 
     total = jnp.sum(total, axis=0, keepdims=True)
-    line = lax.broadcasted_iota(jnp.int32, (META, slots), 0)
-    both = jnp.where(line == 0, peak, jnp.where(line == 1, total, 0.0))
-    colbuf[...] = jnp.transpose(both)
-    my_meta = meta_block(colbuf[:, 0:1], colbuf[:, 1:2])
+    colbuf[0] = jnp.transpose(jnp.broadcast_to(peak, (META, slots)))
+    colbuf[1] = jnp.transpose(jnp.broadcast_to(total, (META, slots)))
+    my_meta = meta_block(colbuf[0], colbuf[1])
 
     def weigh(h):
         cols = pl.ds(pl.multiple_of(h * half, half), half)
@@ -194,12 +197,14 @@
     acc[...] = weigh(c)
     first_copy.wait()
 
-    mine, my_total = colbuf[:, 0:1], colbuf[:, 1:2]
+    mine, my_total = colbuf[0], colbuf[1]
     other, other_total = read_meta(r0[:, half:])
     joint = jnp.maximum(mine, other)
     wa, wb = jnp.exp(mine - joint), jnp.exp(other - joint)
     s1[:, half:] = meta_block(joint, my_total * wa + other_total * wb)
-    s1[:, :half] = (acc[...] * wa + r0[:, :half].astype(F32) * wb).astype(BF16)
+    s1[:, :half] = (
+        acc[...] * wide(wa, half) + r0[:, :half].astype(F32) * wide(wb, half)
+    ).astype(BF16)
 
     order = sorted(range(1, PLANE), key=plane_hops, reverse=True)
     plane_copies = {}
@@ -219,11 +224,12 @@
         cbuf[at, :] = (ex * (1.0 / jnp.sum(ex, axis=1, keepdims=True))).astype(BF16)
 
     def merge(blocks):
-        metas = [read_meta(b[:, half:]) for b in blocks]
-        joint = functools.reduce(jnp.maximum, [m for m, _ in metas])
-        scales = [jnp.exp(m - joint) for m, _ in metas]
-        out = sum(b[:, :half].astype(F32) * w for b, w in zip(blocks, scales))
-        return out, joint, sum(t * w for (_, t), w in zip(metas, scales))
+        peaks, totals = read_meta(jnp.concatenate([b[:, half:] for b in blocks], axis=0))
+        cut = [slice(i * piece, (i + 1) * piece) for i in range(len(blocks))]
+        joint = functools.reduce(jnp.maximum, [peaks[at] for at in cut])
+        scales = [jnp.exp(peaks[at] - joint) for at in cut]
+        out = sum(b[:, :half].astype(F32) * wide(w, half) for b, w in zip(blocks, scales))
+        return out, joint, sum(totals[at] * w for at, w in zip(cut, scales))
 
     for k in order:
         plane_copies[k].wait_recv()
@@ -238,11 +244,13 @@
             s2, r2.at[k], column_send.at[k], column_recv.at[k], column_peer(k)[0]
         )
         column_copies[k].start()
+    for copy in plane_copies.values():
+        copy.wait_send()
     for k in column_order:
         column_copies[k].wait_recv()
     for low in range(2):
         out, _, tot = merge([s2[...] if k == 0 else r2[k] for k in range(low, COLUMN, 2)])
-        sl[c, pl.ds(column_peer(low)[1], piece), :] = (out / tot).astype(BF16)
+        sl[c, pl.ds(column_peer(low)[1], piece), :] = (out / wide(tot, half)).astype(BF16)
     in_copy = remote(sl.at[c], sl.at[c], core_send.at[1], core_recv.at[1], partner)
     in_copy.start()
     win_copy.wait()
@@ -285,6 +293,8 @@
         )
         back_copies[k].start()
     mine = s4[pl.ds(column_peer(0)[1], piece), :].astype(F32)
+    for copy in column_copies.values():
+        copy.wait_send()
     for k in column_order:
         back_copies[k].wait_recv()
     for k in column_order:
@@ -298,6 +308,8 @@
             g_ref.at[c, at], g_ref.at[c, at], gather_send.at[k], gather_recv.at[k], plane_peer(k)[0]
         )
         gathers[k].start()
+    for copy in back_copies.values():
+        copy.wait_send()
     forwards = []
     for k in [0] + order[::-1]:
         if k:
@@ -313,11 +325,10 @@
         begun[at, :] = jnp.dot(
             cbuf[at, :], g_ref[c], preferred_element_type=F32
         ).astype(BF16)
+    for copy in gathers.values():
+        copy.wait_send()
     for copy in forwards:
         copy.wait()
-    for copies in (plane_copies, column_copies, back_copies, gathers):
-        for copy in copies.values():
-            copy.wait_send()
 
 
 def mix_kernel(c_ref, g_ref, begun, o_hbm, obuf, sem, begun_sem):
@@ -374,7 +385,7 @@
             pltpu.VMEM((width, slots), BF16),
             pltpu.VMEM((8, slots), F32),
             pltpu.VMEM((slots, half), F32),
-            pltpu.VMEM((slots, META), F32),
+            pltpu.VMEM((2, slots, META), F32),
             pltpu.VMEM((slots, wide), BF16),
             pltpu.VMEM((slots, wide), BF16),
             pltpu.VMEM((slots, wide), BF16),

time: 46.6 us -> 46.1 us (0.989)
  Pallas kernels: 46.5 us -> 46 us
where the time goes in v8:
time: 46.1 us; the launch traced here: 46 us
  Pallas kernels  46 us (100%)
    pallas_call x1, Pallas kernels, on_device(): pl.pallas_call(moe_kernel, out_shape=(pltpu.VMEM((n, slots), BF16), pltpu...  42.6 us
    pallas_call x1, Pallas kernels, on_device(): pl.pallas_call(mix_kernel, out_shape=jax.ShapeDtypeStruct((n, width), BF1...  3.41 us

profile of v8, /device:TPU:1, one launch (start us, length us, event | category | flops | bytes accessed | tf_op | source)
XLA Modules:
  0.0 46.0 jit_solution(18169382257456923313)
XLA Ops:
  0.0 42.6 %moe.1 = (bf16[4096,256]{1,0:T(8,128)(2,1)S(1)}, bf16[2,256,512]{2,1,0:T(8,128)(2,1)S(1)}, bf16[2048,512]{1,0:T(8,128)(2,1)S(1)}) custom-call(bf16[4096,1024]{1,0:T(8,128)(2,1)} %tok.1, f32[1,1024]{1,0:T(1,128)} %bitcast.1, bf16[1024,256]{1,0:T(8,128)(2,1)} %slot_hbm.1, bf16[8,1024,256]{2,1,0:T(8,128)(2,1)} %win_hbm.1, bf16[8,256,1024]{2,1,0:T(8,128)(2,1)} %wout_hbm.1), custom_call_target="tpu_custom_call" | custom-call | tf_op jit(solution)/shard_map/moe/pallas_call | solution.py:367
  42.6 3.4 %mix.1 = bf16[4096,1024]{1,0:T(8,128)(2,1)} custom-call(bf16[4096,256]{1,0:T(8,128)(2,1)S(1)} %get-tuple-element.8.c_ref, bf16[2,256,512]{2,1,0:T(8,128)(2,1)S(1)} %get-tuple-element.9.g_ref, bf16[2048,512]{1,0:T(8,128)(2,1)S(1)} %get-tuple-element.10.begun), custom_call_target="tpu_custom_call" | custom-call | tf_op jit(solution)/shard_map/mix/pallas_call | solution.py:420

commit v9 on v8

--- a/solution.py
+++ b/solution.py
@@ -231,7 +231,7 @@
         out = sum(b[:, :half].astype(F32) * wide(w, half) for b, w in zip(blocks, scales))
         return out, joint, sum(totals[at] * w for at, w in zip(cut, scales))
 
-    for k in order:
+    for k in order[::-1]:
         plane_copies[k].wait_recv()
     summed, joint, total_k = merge([s1[pl.ds(my_row, piece), :]] + [r1[k] for k in range(1, PLANE)])
     s2[:, :half] = summed.astype(BF16)
@@ -246,7 +246,7 @@
         column_copies[k].start()
     for copy in plane_copies.values():
         copy.wait_send()
-    for k in column_order:
+    for k in column_order[::-1]:
         column_copies[k].wait_recv()
     for low in range(2):
         out, _, tot = merge([s2[...] if k == 0 else r2[k] for k in range(low, COLUMN, 2)])
@@ -295,7 +295,7 @@
     mine = s4[pl.ds(column_peer(0)[1], piece), :].astype(F32)
     for copy in column_copies.values():
         copy.wait_send()
-    for k in column_order:
+    for k in column_order[::-1]:
         back_copies[k].wait_recv()
     for k in column_order:
         mine += r4[k].astype(F32)

time: 46.1 us -> 46.1 us (level)
  no operation moved by 1% of the time
where the time goes in v9:
time: 46.1 us; the launch traced here: 46 us
  Pallas kernels  46 us (100%)
    pallas_call x1, Pallas kernels, on_device(): pl.pallas_call(moe_kernel, out_shape=(pltpu.VMEM((n, slots), BF16), pltpu...  42.6 us
    pallas_call x1, Pallas kernels, on_device(): pl.pallas_call(mix_kernel, out_shape=jax.ShapeDtypeStruct((n, width), BF1...  3.41 us

profile of v9, /device:TPU:1, one launch (start us, length us, event | category | flops | bytes accessed | tf_op | source)
XLA Modules:
  0.0 46.0 jit_solution(12119489936397561052)
XLA Ops:
  0.0 42.6 %moe.1 = (bf16[4096,256]{1,0:T(8,128)(2,1)S(1)}, bf16[2,256,512]{2,1,0:T(8,128)(2,1)S(1)}, bf16[2048,512]{1,0:T(8,128)(2,1)S(1)}) custom-call(bf16[4096,1024]{1,0:T(8,128)(2,1)} %tok.1, f32[1,1024]{1,0:T(1,128)} %bitcast.1, bf16[1024,256]{1,0:T(8,128)(2,1)} %slot_hbm.1, bf16[8,1024,256]{2,1,0:T(8,128)(2,1)} %win_hbm.1, bf16[8,256,1024]{2,1,0:T(8,128)(2,1)} %wout_hbm.1), custom_call_target="tpu_custom_call" | custom-call | tf_op jit(solution)/shard_map/moe/pallas_call | solution.py:367
  42.6 3.4 %mix.1 = bf16[4096,1024]{1,0:T(8,128)(2,1)} custom-call(bf16[4096,256]{1,0:T(8,128)(2,1)S(1)} %get-tuple-element.8.c_ref, bf16[2,256,512]{2,1,0:T(8,128)(2,1)S(1)} %get-tuple-element.9.g_ref, bf16[2048,512]{1,0:T(8,128)(2,1)S(1)} %get-tuple-element.10.begun), custom_call_target="tpu_custom_call" | custom-call | tf_op jit(solution)/shard_map/mix/pallas_call | solution.py:420
